TPU v7x, 512 devices: a whole 4x4x16 slice. The times are simulated.
512 devices in a mesh: grp: 16 (over y, x), tile: 32 (over z, core).
Axes of the slice: x: 4, y: 4, z: 16, core: 2. Of those that a mesh axis runs over, the one named last changes fastest.
Arguments:
- jac_point: float32 [6, 2097152], P(None, ('grp', 'tile')), may hold values from -6 to 6
- jac_cam: float32 [18, 2097152], P(None, ('grp', 'tile')), may hold values from -3 to 3
- resid: float32 [2, 2097152], P(None, ('grp', 'tile')), may hold values from -6 to 6
- point_index: int32 [2097152], P(('grp', 'tile')), may hold values from 0 to 4095, as said below
- cam_index: int32 [2097152], P(('grp', 'tile')), may hold values from 0 to 12287, as said below
Outputs:
- point_step: float32 [3, 2097152], P(None, ('grp', 'tile'))
- camera_step: float32 [9, 196608], P(None, ('grp', 'tile'))
- point_resid: float32 [3, 2097152], P(None, ('grp', 'tile'))
- camera_resid: float32 [9, 196608], P(None, ('grp', 'tile'))
Inputs may be any that keep to these rules, and one draw needn't show every extreme that they name: `point_index`: index among the points of the observation's own device; every device names point 0 and point 4096 - 1. `cam_index`: block h of a device's observations (slots h * 256 to (h + 1) * 256 - 1) names cameras of group h by their index within the group; every block names camera 0 and camera 12288 - 1.
All inputs are finite; a program needn't handle non-finite values.
Results may differ from a plain program's by a relative error of at most 0.0002.
Values sent between devices are 32-bit elements; how exact they have to be, the bound alone decides.
A program may use at most 64 MiB of HBM per device.

v0:
```python
import jax
import jax.numpy as jnp
from jax import lax
from jax.sharding import PartitionSpec as P

P_DEV = 4096
CAM_DEV = 384
ITERS = 2


damping = 1.0


def segment_rows(data, ids, count):
    return jax.vmap(lambda row: jax.ops.segment_sum(row, ids, num_segments=count))(data)


def shards(jac_point, jac_cam, resid, point_index, cam_index):
    obs_dev = jac_point.shape[1]
    cam_grp = CAM_DEV * lax.axis_size("tile")
    jp = jac_point.reshape(2, 3, obs_dev)
    jc = jac_cam.reshape(2, 9, obs_dev)
    owned_index = lax.all_to_all(cam_index, "grp", split_axis=0, concat_axis=0, tiled=True)
    point_rhs = segment_rows(-jnp.sum(jp * resid[:, None], axis=0), point_index, P_DEV)
    point_diag = segment_rows(jnp.sum(jp * jp, axis=0), point_index, P_DEV)
    grad_terms, square_terms = (
        lax.all_to_all(
            -jnp.sum(jc * resid[:, None], axis=0), "grp", split_axis=1, concat_axis=1, tiled=True
        ),
        lax.all_to_all(jnp.sum(jc * jc, axis=0), "grp", split_axis=1, concat_axis=1, tiled=True),
    )
    group_terms = segment_rows(
        jnp.concatenate([grad_terms, square_terms], axis=0), owned_index, cam_grp
    )
    camera_both = lax.psum_scatter(group_terms, "tile", scatter_dimension=1, tiled=True)
    camera_rhs, camera_diag = (camera_both[:9], camera_both[9:])

    def inner(ap, ac, bp, bc):
        return jnp.sum(ap * bp) + jnp.sum(ac * bc)

    def norm_sum(rp, rc, zp, zc):
        return lax.psum(inner(rp, rc, zp, zc), ("grp", "tile"))

    point_pre = point_diag + damping
    camera_pre = camera_diag + damping
    point_x = jnp.zeros_like(point_rhs)
    camera_x = jnp.zeros_like(camera_rhs)
    point_r, camera_r = (point_rhs, camera_rhs)
    point_z, camera_z = (point_r / point_pre, camera_r / camera_pre)
    point_dir, camera_dir = (point_z, camera_z)
    norm_now = norm_sum(point_r, camera_r, point_z, camera_z)
    for step_number in range(ITERS):
        group_cams = lax.all_gather(camera_dir, "tile", axis=1, tiled=True)
        fetched = group_cams[:, owned_index]
        point_term = jnp.sum(jp * point_dir[:, point_index][None], axis=1)
        at_obs = lax.all_to_all(fetched, "grp", split_axis=1, concat_axis=1, tiled=True)
        error = point_term + jnp.sum(jc * at_obs[None], axis=1)
        column = lax.all_to_all(
            jnp.sum(jc * error[:, None], axis=0), "grp", split_axis=1, concat_axis=1, tiled=True
        )
        camera_out = lax.psum_scatter(
            segment_rows(column, owned_index, cam_grp), "tile", scatter_dimension=1, tiled=True
        )
        point_out = segment_rows(jnp.sum(jp * error[:, None], axis=0), point_index, P_DEV)
        point_q = point_out + damping * point_dir
        camera_q = camera_out + damping * camera_dir
        curve = lax.psum(inner(point_dir, camera_dir, point_q, camera_q), ("grp", "tile"))
        alpha = norm_now / curve
        point_x = point_x + alpha * point_dir
        camera_x = camera_x + alpha * camera_dir
        point_r = point_r - alpha * point_q
        camera_r = camera_r - alpha * camera_q
        if step_number + 1 < ITERS:
            point_z, camera_z = (point_r / point_pre, camera_r / camera_pre)
            norm_next = norm_sum(point_r, camera_r, point_z, camera_z)
            ratio = norm_next / norm_now
            point_dir = point_z + ratio * point_dir
            camera_dir = camera_z + ratio * camera_dir
            norm_now = norm_next
    return (point_x, camera_x, point_r, camera_r)


def solution(mesh):
    placed = (
        P(None, ("grp", "tile")),
        P(None, ("grp", "tile")),
        P(None, ("grp", "tile")),
        P(("grp", "tile")),
        P(("grp", "tile")),
    )
    return jax.shard_map(
        shards,
        mesh=mesh,
        in_specs=placed,
        out_specs=(
            P(None, ("grp", "tile")),
            P(None, ("grp", "tile")),
            P(None, ("grp", "tile")),
            P(None, ("grp", "tile")),
        ),
        check_vma=False,
    )
```

profile of v0, /device:TPU:1, one launch (start us, length us, event | category | flops | bytes accessed | tf_op | source)
XLA Modules:
  0.0 1094.1 jit_solution(12470036015440183946)
XLA Ops:
  10.1 7.6 all-to-all-start.1
  18.5 6.8 all-to-all-done.1
  25.3 3.5 all-to-all-start.2
  29.3 7.1 all-to-all-done.2
  36.4 3.5 all-to-all-start
  40.9 5.3 all-to-all-done
  46.3 25.4 %scatter_custom_fusion.2 = f32[18,12288]{0,1:T(8,128)} fusion(s32[4096]{0:T(1024)S(1)} %bitcast.80, f32[4096,18]{1,0:T(8,128)S(1)} %copy.50, f32[]{:T(128)} %constant.5.clone.1), kind=kCustom, calls=%fused_computation.15 | custom fusion | flops 73728 | bytes 884740 | tf_op jit(solution)/shard_map/vmap()/scatter-add | solution.py:15
  71.7 119.8 %reduce-scatter.4.cloned.1.call-done = f32[18,384]{0,1:T(8,128)} async-done(((f32[18,12288]{0,1:T(8,128)}), f32[18,384]{0,1:T(8,128)}) %reduce-scatter.4.cloned.1.call-update) | async-done | bytes 27664 | tf_op jit(solution)/shard_map/reduce_scatter | solution.py:35
  192.7 57.6 %all_gather.6 = f32[9,12288]{0,1:T(8,128)} all-gather(f32[9,384]{0,1:T(8,128)S(1)} %fusion.11), channel_id=1, replica_groups=mesh['grp'=16,'tile'=32] {'tile'}, dimensions={1}, use_global_device_ids=true | all-gather | bytes 456192 | tf_op jit(solution)/shard_map/all_gather | solution.py:53
  250.3 13.6 %gather_fusion.1 = f32[4096,9]{1,0:T(8,128)S(1)} fusion(f32[9,12288]{0,1:T(8,128)} %all_gather.6, s32[4096]{0:T(1024)S(1)} %broadcast_clamp_fusion), kind=kCustom, calls=%fused_computation.1 | custom fusion | bytes 311296 | tf_op jit(solution)/shard_map/gather | solution.py:54
  265.2 6.4 all-to-all-start.3
  272.3 23.8 %scatter_custom_fusion = f32[3,4096]{0,1:T(8,128)} fusion(s32[4096]{0:T(1024)S(1)} %copy-done.5, f32[4096,3]{1,0:T(8,128)S(1)} %copy.43, f32[]{:T(128)} %constant.5.clone.1), kind=kCustom, calls=%fused_computation.27 | custom fusion | flops 12288 | bytes 49156 | tf_op jit(solution)/shard_map/vmap()/scatter-add | solution.py:15
  296.8 23.7 %scatter_custom_fusion.1 = f32[3,4096]{0,1:T(8,128)} fusion(s32[4096]{0:T(1024)S(1)} %copy-done.5, f32[4096,3]{1,0:T(8,128)S(1)} %copy.44, f32[]{:T(128)} %constant.6.clone.1), kind=kCustom, calls=%fused_computation.25 | custom fusion | flops 12288 | bytes 49156 | tf_op jit(solution)/shard_map/vmap()/scatter-add | solution.py:15
  323.0 14.2 %gather_fusion = f32[4096,3]{1,0:T(8,128)} fusion(f32[3,4096]{0,1:T(8,128)S(1)} %div.21, s32[4096]{0:T(1024)S(1)} %fusion.12), kind=kCustom, calls=%fused_computation | custom fusion | bytes 114688 | tf_op jit(solution)/shard_map/gather | solution.py:55
  340.2 14.0 %all_to_all.72 = f32[9,16,256]{2,0,1:T(8,128)S(1)} all-to-all(f32[9,16,256]{2,0,1:T(8,128)S(1)} %copy.55), channel_id=1, replica_groups=mesh['grp'=16,'tile'=32] {'grp'}, dimensions={1} | all-to-all | bytes 294912 | tf_op jit(solution)/shard_map/all_to_all | solution.py:58
  356.5 25.7 %scatter_custom_fusion.4 = f32[9,12288]{0,1:T(8,128)} fusion(s32[4096]{0:T(1024)S(1)} %bitcast.82, f32[4096,9]{1,0:T(8,128)} %copy.57, f32[]{:T(128)} %constant.5.clone.1), kind=kCustom, calls=%fused_computation.13 | custom fusion | flops 36864 | bytes 442880 | tf_op jit(solution)/shard_map/vmap()/scatter-add | solution.py:15
  384.3 23.4 %scatter_fusion = f32[3,4096]{0,1:T(8,128)S(1)} fusion(f32[3,4096]{0,1:T(8,128)S(1)} %copy-done.2, s32[4096]{0:T(1024)S(1)} %copy-done.5, f32[4096,3]{1,0:T(8,128)} %copy.54), kind=kCustom, calls=%fused_computation.7 | custom fusion | flops 12288 | bytes 163840 | tf_op jit(solution)/shard_map/vmap()/scatter-add | solution.py:15
  407.8 3.5 multiply_reduce_fusion.2
  411.2 82.1 %reduce-scatter.6.cloned.1.call-done = f32[9,384]{0,1:T(8,128)} async-done(((f32[9,12288]{0,1:T(8,128)}), f32[9,384]{0,1:T(8,128)}) %reduce-scatter.6.cloned.1.call-update) | async-done | bytes 13840 | tf_op jit(solution)/shard_map/reduce_scatter | solution.py:61
  497.6 106.1 %all-reduce = (f32[]{:T(128)}, f32[]{:T(128)}) all-reduce(f32[]{:T(128)S(6)} %add.103, f32[]{:T(128)S(6)} %add.108), channel_id=1, replica_groups=mesh['grp'=16,'tile'=32] {'grp','tile'}, use_global_device_ids=true, to_apply=%region_10.0 | all-reduce | flops 2 | bytes 16 | tf_op jit(solution)/shard_map/psum | solution.py:42
  605.1 5.3 multiply_reduce_fusion.1
  612.4 98.6 %psum.30 = f32[]{:T(128)} all-reduce(f32[]{:T(128)S(6)} %add.109), channel_id=1, replica_groups=mesh['grp'=16,'tile'=32] {'grp','tile'}, use_global_device_ids=true, to_apply=%region_23.0 | all-reduce | flops 1 | bytes 8 | tf_op jit(solution)/shard_map/psum | solution.py:42
  712.4 53.7 %all_gather.7 = f32[9,12288]{0,1:T(8,128)} all-gather(f32[9,384]{0,1:T(8,128)S(1)} %multiply_add_fusion.3), channel_id=1, replica_groups=mesh['grp'=16,'tile'=32] {'tile'}, dimensions={1}, use_global_device_ids=true | all-gather | bytes 456192 | tf_op jit(solution)/shard_map/all_gather | solution.py:53
  766.1 17.0 %gather_fusion.3 = f32[4096,9]{1,0:T(8,128)} fusion(f32[9,12288]{0,1:T(8,128)} %all_gather.7, s32[4096]{0:T(1024)S(1)} %broadcast_clamp_fusion), kind=kCustom, calls=%fused_computation.3 | custom fusion | bytes 311296 | tf_op jit(solution)/shard_map/gather | solution.py:54
  786.1 4.2 all-to-all-start.5
  793.7 15.7 %gather_fusion.2 = f32[4096,3]{1,0:T(8,128)} fusion(f32[3,4096]{0,1:T(8,128)} %multiply_add_fusion.1, s32[4096]{0:T(1024)S(1)} %fusion.12), kind=kCustom, calls=%fused_computation.2 | custom fusion | bytes 114688 | tf_op jit(solution)/shard_map/gather | solution.py:55
  813.3 14.4 %all_to_all.73 = f32[9,16,256]{2,0,1:T(8,128)S(1)} all-to-all(f32[9,16,256]{2,0,1:T(8,128)S(1)} %copy.62), channel_id=1, replica_groups=mesh['grp'=16,'tile'=32] {'grp'}, dimensions={1} | all-to-all | bytes 294912 | tf_op jit(solution)/shard_map/all_to_all | solution.py:58
  830.0 25.7 %scatter_custom_fusion.6 = f32[9,12288]{0,1:T(8,128)} fusion(s32[4096]{0:T(1024)S(1)} %bitcast.83, f32[4096,9]{1,0:T(8,128)} %copy.64, f32[]{:T(128)} %constant.5.clone.1), kind=kCustom, calls=%fused_computation.11 | custom fusion | flops 36864 | bytes 442880 | tf_op jit(solution)/shard_map/vmap()/scatter-add | solution.py:15
  860.8 23.3 %scatter_fusion.1 = f32[3,4096]{0,1:T(8,128)} fusion(f32[3,4096]{0,1:T(8,128)} %copy.80, s32[4096]{0:T(1024)S(1)} %copy-done.5, f32[4096,3]{1,0:T(8,128)} %copy.61), kind=kCustom, calls=%fused_computation.9 | custom fusion | flops 12288 | bytes 163840 | tf_op jit(solution)/shard_map/vmap()/scatter-add | solution.py:15
  887.4 78.7 %reduce-scatter.8.cloned.1.call-done = f32[9,384]{0,1:T(8,128)} async-done(((f32[9,12288]{0,1:T(8,128)}), f32[9,384]{0,1:T(8,128)}) %reduce-scatter.8.cloned.1.call-update) | async-done | bytes 13840 | tf_op jit(solution)/shard_map/reduce_scatter | solution.py:61
  969.0 106.2 %psum.31 = f32[]{:T(128)} all-reduce(f32[]{:T(128)S(6)} %add.114), channel_id=1, replica_groups=mesh['grp'=16,'tile'=32] {'grp','tile'}, use_global_device_ids=true, to_apply=%region_33.0 | all-reduce | flops 1 | bytes 8 | tf_op jit(solution)/shard_map/psum | solution.py:67
  1078.0 5.3 multiply_subtract_fusion
  (99 shorter events, 49.7 us)
Async XLA Ops:
  9.1 19.8 %copy-start.7 = (f32[6,4096]{1,0:T(8,128)S(1)}, f32[6,4096]{1,0:T(8,128)}, u32[]{:S(2)}) copy-start(f32[6,4096]{1,0:T(8,128)} %param.5) | copy-start | bytes 294916
  9.1 19.8 %copy-start.6 = (f32[2,4096]{1,0:T(2,128)S(1)}, f32[2,4096]{1,0:T(2,128)}, u32[]{:S(2)}) copy-start(f32[2,4096]{1,0:T(2,128)} %param.7) | copy-start | bytes 98308
  10.1 15.3 %all-to-all-start.1 = ((f32[9,16,256]{2,0,1:T(8,128)}), f32[9,16,256]{2,0,1:T(8,128)S(1)}, u32[]{:S(2)}, u32[]{:S(2)}) async-start(f32[9,16,256]{2,0,1:T(8,128)} %copy.46), calls=%async_computation.1 | async-start | bytes 524288 | tf_op jit(solution)/shard_map/all_to_all | solution.py:27
  25.3 11.0 %all-to-all-start.2 = ((f32[9,16,256]{2,0,1:T(8,128)}), f32[9,16,256]{2,0,1:T(8,128)S(1)}, u32[]{:S(2)}, u32[]{:S(2)}) async-start(f32[9,16,256]{2,0,1:T(8,128)} %copy.48), calls=%async_computation.2 | async-start | bytes 524288 | tf_op jit(solution)/shard_map/all_to_all | solution.py:30
  36.4 9.9 all-to-all-start
  39.9 151.6 %reduce-scatter.4.cloned.1.call-start = ((), (), s32[]{:S(2)}) async-start(), calls=%async_computation.10 | async-start | bytes 6488064 | tf_op jit(solution)/shard_map/reduce_scatter | solution.py:35
  250.2 21.4 %copy-start.5 = (s32[4096]{0:T(1024)S(1)}, s32[4096]{0:T(1024)}, u32[]{:S(2)}) copy-start(s32[4096]{0:T(1024)} %param.8) | copy-start | bytes 49156
  265.2 74.4 %all-to-all-start.3 = ((f32[9,16,256]{2,0,1:T(8,128)}), f32[9,16,256]{2,0,1:T(8,128)S(1)}, u32[]{:S(2)}, u32[]{:S(2)}) async-start(f32[9,16,256]{2,0,1:T(8,128)} %copy.52), calls=%async_computation.4 | async-start | bytes 524288 | tf_op jit(solution)/shard_map/all_to_all | solution.py:56
  271.6 221.7 %reduce-scatter.6.cloned.1.call-start = ((), (), s32[]{:S(2)}) async-start(), calls=%async_computation.11 | async-start | bytes 6488064 | tf_op jit(solution)/shard_map/reduce_scatter | solution.py:61
  323.0 59.2 %copy-start = (f32[3,4096]{0,1:T(8,128)}, f32[3,4096]{0,1:T(8,128)S(1)}, u32[]{:S(2)}) copy-start(f32[3,4096]{0,1:T(8,128)S(1)} %div.21) | copy-start | bytes 147460
  382.2 2.1 copy-start.2
  407.8 85.6 %copy-start.3 = (f32[18,384]{0,1:T(8,128)S(1)}, f32[18,384]{0,1:T(8,128)}, u32[]{:S(2)}) copy-start(f32[18,384]{0,1:T(8,128)} %reduce-scatter.4.cloned.1.call-done) | copy-start | bytes 82948
  766.1 24.4 %copy-start.1 = (f32[3,4096]{0,1:T(8,128)S(1)}, f32[3,4096]{0,1:T(8,128)}, u32[]{:S(2)}) copy-start(f32[3,4096]{0,1:T(8,128)} %copy-done) | copy-start | bytes 147460
  786.1 25.6 %all-to-all-start.5 = ((f32[9,16,256]{2,0,1:T(8,128)}), f32[9,16,256]{2,0,1:T(8,128)}, u32[]{:S(2)}, u32[]{:S(2)}) async-start(f32[9,16,256]{2,0,1:T(8,128)} %copy.59), calls=%async_computation.7 | async-start | bytes 524288 | tf_op jit(solution)/shard_map/all_to_all | solution.py:56
  790.3 175.8 %reduce-scatter.8.cloned.1.call-start = ((), (), s32[]{:S(2)}) async-start(), calls=%async_computation.12 | async-start | bytes 6488064 | tf_op jit(solution)/shard_map/reduce_scatter | solution.py:61
  1083.3 3.0 copy-start.4
Sparse Core Ops, SparseCore 0:
  71.8 119.6 reduce-scatter.3
  382.4 110.9 reduce-scatter.5
  855.8 110.2 reduce-scatter.7
where the time goes:
time: 1100 us; the launch traced here: 1090 us
  blocking collectives  451 us (41%)
  waiting for transfers between devices  300 us (27%)
  other arithmetic  201 us (18%)
  local copies, waits for them, and re-layouts  93.5 us (8%)
  starting transfers between devices  25.5 us (2%)
  between operations  23.5 us (2%)
    psum x2, blocking collectives, norm_sum(): return lax.psum(inner(rp, rc, zp, zc), ('grp', 'tile'))  205 us
    scatter-add x7, other arithmetic, segment_rows(): jax.ops.segment_sum(row, ids, num_segments=count)  171 us
    reduce_scatter x2, waiting for transfers between devices, shards(): lax.psum_scatter(segment_rows(column, owned_index, cam_grp), 'tile', scat...  161 us
    reduce_scatter x1, waiting for transfers between devices, shards(): lax.psum_scatter(group_terms, 'tile', scatter_dimension=1, tiled=True)  120 us
    all_gather x2, blocking collectives, shards(): group_cams = lax.all_gather(camera_dir, 'tile', axis=1, tiled=True)  111 us
    psum x1, blocking collectives, shards(): lax.psum(inner(point_dir, camera_dir, point_q, camera_q), ('grp', 'tile'))  106 us
    gather x4, local copies, waits for them, and re-layouts, shards(): point_term = jnp.sum(jp * point_dir[:, point_index][None], axis=1)  34.3 us
    gather x2, local copies, waits for them, and re-layouts, shards(): fetched = group_cams[:, owned_index]  30.6 us
  transfers between devices with their start and end apart: 8, of which 6 were waited for; matrix products, arithmetic and copies ran while one was open for 14% of the time, Pallas kernels for 0%

commit v1 on v0

v1 whole, which is shorter than its diff:
```python
import functools

import jax
import jax.numpy as jnp
from jax import lax
from jax.experimental import pallas as pl
from jax.experimental.pallas import tpu as pltpu
from jax.sharding import PartitionSpec as P

F32, BF16, I32 = jnp.float32, jnp.bfloat16, jnp.int32
MESH = pl.DeviceIdType.MESH
SLOT = 256
CAM_DEV = 384
damping = 1.0


def spread(n, d):
    half = lax.div(d + 1, jnp.int32(2))
    return half * (2 * lax.rem(d, jnp.int32(2)) - 1) + n


def kernel(
    NG, OBS, NPTS,
    jp, jc, res, pidx, cidx,
    xp, xc, rp, rc,
    S, R2, OHC, OHP, LHS, LHSP, ACC, AROW, APROW, TV, TP,
    SB0, RB0, SB, RB, VB, CV, PV, PVEC,
    PTS, PTR, XS, XR, ER, EB, G, GZ, GP, XF, XG,
    loc, a2a_s, a2a_r, fwd_s, fwd_r, rs_s, rs_r, ag_s, ag_r,
    pt_s, pt_r, x_s, x_r, e_s, e_r, gz_s, gz_r, gp_s, gp_r, gq_s, gq_r, pm_s, pm_r,
):
    T = NG // 2
    ROWS = T * 32
    NA = NPTS // 256
    one = jnp.int32(1)
    ng = jnp.int32(NG)
    g = lax.axis_index("grp")
    tt = lax.axis_index("tile")
    z = lax.div(tt, jnp.int32(2))
    c = lax.rem(tt, jnp.int32(2))
    partner = (g, 2 * z + 1 - c)

    def z_at(k):
        d = lax.rem(ng - k, ng)
        return lax.rem(z + spread(ng, d), ng)

    def g_at(d):
        return lax.rem(g + d, ng)

    bar = pltpu.get_barrier_semaphore()

    @pl.loop(1, NG)
    def _(d):
        pl.semaphore_signal(bar, inc=1, device_id=(g, 2 * z_at(d) + c), device_id_type=MESH)
        pl.semaphore_signal(bar, inc=1, device_id=(g_at(d), tt), device_id_type=MESH)

    pl.semaphore_signal(bar, inc=1, device_id=partner, device_id_type=MESH)

    @pl.when(g != z)
    def _():
        pl.semaphore_signal(bar, inc=1, device_id=(z, 2 * g + c), device_id_type=MESH)

    @pl.loop(0, NG)
    def _(h):
        cols = pl.ds(pl.multiple_of(h * SLOT, SLOT), SLOT)
        S[h, 0:8, :] = jc[0:8, cols]
        S[h, 8:16, :] = jc[9:17, cols]
        S[h, 16:17, :] = jc[8:9, cols]
        S[h, 17:18, :] = jc[17:18, cols]
        S[h, 18:20, :] = res[:, cols]
        S[h, 20:21, :] = cidx[:, cols].astype(F32)

    G[...] = jnp.zeros_like(G)

    pl.semaphore_wait(bar, 2 * (NG - 1) + 1 + jnp.where(g != z, 1, 0))

    def a2a_copy(zt, zf):
        return pltpu.make_async_remote_copy(
            S.at[zt], R2.at[c, zf], a2a_s.at[zt], a2a_r.at[zf],
            device_id=(g, 2 * zt + c), device_id_type=MESH)

    own = pltpu.make_async_copy(S.at[z], R2.at[c, z], loc)
    own.start()

    @pl.loop(1, NG)
    def _(k):
        a2a_copy(z_at(k), z).start()

    def fold(v):
        out = v[:, 0:128]
        for i in range(1, v.shape[1] // 128):
            out = out + v[:, i * 128:(i + 1) * 128]
        return jnp.sum(out, axis=0, keepdims=True)

    def point_lhs(row0, cols, v, ap):
        v2 = jnp.concatenate([v, v], axis=0)
        low = lax.broadcasted_iota(I32, (16, SLOT), 0) < 8
        am = jnp.broadcast_to(ap, (16, SLOT)) - jnp.where(low, 0.0, 1.0)
        for i in range(NA // 2):
            LHSP[row0 + i * 16:row0 + i * 16 + 16, cols] = jnp.where(
                am == float(2 * i), v2, 0.0).astype(BF16)

    def split(v):
        hi = v.astype(BF16).astype(F32)
        return hi, v - hi

    nt = (((1,), (1,)), ((), ()))

    def point_sum(row0):
        out = lax.dot_general(LHSP[row0:row0 + NA * 8, :], OHP[...], nt,
                              preferred_element_type=F32)
        for a in range(NA):
            PV[:, a * 256:(a + 1) * 256] = out[a * 8:(a + 1) * 8, :]

    def point_gather(src, it):
        for i in range(NA // 2):
            parts = []
            for a in (2 * i, 2 * i + 1):
                hi, lo = split(PVEC[src, :, a * 256:(a + 1) * 256])
                parts += [hi, lo, jnp.zeros((2, 256), F32)]
            TP[i * 16:i * 16 + 16, :] = jnp.concatenate(parts, axis=0).astype(BF16)

        @pl.loop(0, NG)
        def _(k):
            h = z_at(k)
            cols = pl.ds(pl.multiple_of(h * SLOT, SLOT), SLOT)
            got = jnp.dot(TP[...], OHP[:, cols], preferred_element_type=F32)
            ap = jnp.broadcast_to(APROW[:, cols], (8, SLOT))
            acc = jnp.zeros((8, SLOT), F32)
            for a in range(NA):
                acc = jnp.where(ap == float(a), got[a * 8:(a + 1) * 8, :], acc)
            v = acc[0:3] + acc[3:6]
            PTS[it, h, :, 0:SLOT] = jnp.sum(jp[0:3, cols] * v, axis=0, keepdims=True)
            PTS[it, h, :, SLOT:2 * SLOT] = jnp.sum(jp[3:6, cols] * v, axis=0, keepdims=True)

            @pl.when(h != z)
            def _():
                pt_copy(it, h, z).start()

            @pl.when(h == z)
            def _():
                pltpu.make_async_copy(PTS.at[it, h], PTR.at[it, z], pt_r.at[it, z]).start()

    def pt_copy(it, zt, zf):
        return pltpu.make_async_remote_copy(
            PTS.at[it, zt], PTR.at[it, zf], pt_s.at[it, zt], pt_r.at[it, zf],
            device_id=(g, 2 * zt + c), device_id_type=MESH)

    @pl.loop(0, NG)
    def _(h):
        cols = pl.ds(pl.multiple_of(h * SLOT, SLOT), SLOT)
        p = pidx[:, cols]
        ap = lax.shift_right_logical(p, 8).astype(F32)
        n = (p & 255).astype(F32)
        APROW[:, cols] = ap
        row = lax.broadcasted_iota(I32, (256, SLOT), 0).astype(F32)
        OHP[:, cols] = jnp.where(row == jnp.broadcast_to(n, (256, SLOT)), 1.0, 0.0).astype(BF16)
        j0, j1 = jp[0:3, cols], jp[3:6, cols]
        s0, s1 = res[0:1, cols], res[1:2, cols]
        v = jnp.concatenate(
            [-(j0 * s0 + j1 * s1), j0 * j0 + j1 * j1, jnp.zeros((2, SLOT), F32)], axis=0)
        hi, lo = split(v)
        point_lhs(0, cols, hi, ap)
        point_lhs(NA * 8, cols, lo, ap)

    out = lax.dot_general(LHSP[...], OHP[...], nt, preferred_element_type=F32)
    for a in range(NA):
        PV[:, a * 256:(a + 1) * 256] = (
            out[a * 8:(a + 1) * 8, :] + out[(NA + a) * 8:(NA + a + 1) * 8, :])
    prhs = PV[0:3, :]
    pmat = PV[3:6, :] + damping
    pz = prhs / pmat
    PVEC[0] = prhs
    PVEC[1] = pmat
    PVEC[2] = pz
    G[0:1, :] += fold(prhs * pz)
    G[1:2, :] += fold(pz * pz)
    point_gather(2, 0)

    pat_row = lax.broadcasted_iota(I32, (32, SLOT), 0)
    pat = jnp.where(pat_row < 8, 0, jnp.where(
        pat_row < 16, 1, jnp.where(
            pat_row < 24, 2, jnp.where(pat_row < 27, pat_row - 24, 2000)))).astype(F32)

    def cam_lhs(row0, col0, v8, v1, am):
        h8, l8 = split(v8)
        h1, l1 = split(v1)
        h1 = jnp.broadcast_to(h1, (8, SLOT))
        l1 = jnp.broadcast_to(l1, (8, SLOT))
        hi = jnp.concatenate([h8, h8, h8, h1], axis=0)
        lo = jnp.concatenate([l8, l8, l8, l1], axis=0)
        for t in range(T):
            hit = am == float(3 * t)
            LHS[row0 + t * 32:row0 + t * 32 + 32, col0:col0 + SLOT] = (
                jnp.where(hit, hi, 0.0).astype(BF16))
            LHS[row0 + ROWS + t * 32:row0 + ROWS + t * 32 + 32, col0:col0 + SLOT] = (
                jnp.where(hit, lo, 0.0).astype(BF16))

    def jac(core, zs):
        return (R2[core, zs, 0:8, :], R2[core, zs, 8:16, :],
                R2[core, zs, 16:17, :], R2[core, zs, 17:18, :])

    def block(zs):
        return pl.ds(pl.multiple_of(zs * (2 * SLOT), 2 * SLOT), 2 * SLOT)

    def half_block(zs, core):
        return pl.ds(pl.multiple_of(zs * (2 * SLOT) + core * SLOT, SLOT), SLOT)

    def fwd_copy(core, zs):
        return pltpu.make_async_remote_copy(
            R2.at[core, zs], R2.at[core, zs], fwd_s.at[zs], fwd_r.at[zs],
            device_id=partner, device_id_type=MESH)

    ACC[...] = jnp.zeros_like(ACC)
    own.wait()
    fwd_copy(c, z).start()
    log_t = T.bit_length() - 1

    @pl.loop(0, NG)
    def _(k):
        @pl.when(k + 1 < NG)
        def _():
            zn = z_at(k + 1)
            a2a_copy(zn, zn).wait_recv()
            fwd_copy(c, zn).start()

        zs = z_at(k)
        fwd_copy(1 - c, zs).wait_recv()
        for core in range(2):
            idx = R2[core, zs, 20:21, :].astype(I32)
            q = lax.shift_right_logical(idx, 7)
            t = lax.shift_right_logical(q * 171, 9)
            tau = lax.shift_right_logical(t, 1)
            a = 3 * (tau & (T - 1)) + (q - 3 * t)
            a = jnp.where((t & 1) == c, a, -1000).astype(F32)
            n = (lax.shift_right_logical(tau, log_t) * 128 + (idx & 127)).astype(F32)
            AROW[:, half_block(zs, core)] = a
            row = lax.broadcasted_iota(I32, (256, SLOT), 0).astype(F32)
            OHC[:, half_block(zs, core)] = jnp.where(
                row == jnp.broadcast_to(n, (256, SLOT)), 1.0, 0.0).astype(BF16)
            am = jnp.broadcast_to(a, (32, SLOT)) - pat
            J0, J1, j0, j1 = jac(core, zs)
            s0, s1 = R2[core, zs, 18:19, :], R2[core, zs, 19:20, :]
            cam_lhs(0, core * SLOT, -(J0 * s0 + J1 * s1), -(j0 * s0 + j1 * s1), am)
            cam_lhs(2 * ROWS, core * SLOT, J0 * J0 + J1 * J1, j0 * j0 + j1 * j1, am)
        ACC[...] += lax.dot_general(LHS[...], OHC[:, block(zs)], nt, preferred_element_type=F32)

    def rs_copy(it, gt, gf):
        if it == 2:
            src, dst = SB0.at[gt], RB0.at[gf]
        else:
            src, dst = SB.at[it, gt], RB.at[it, gf]
        return pltpu.make_async_remote_copy(
            src, dst, rs_s.at[it, gt], rs_r.at[it, gf],
            device_id=(gt, tt), device_id_type=MESH)

    def rs_start(it):
        @pl.loop(1, NG)
        def _(d):
            rs_copy(it, g_at(d), g).start()

    for half in range(2):
        lanes = slice(half * 128, half * 128 + 128)
        for t in range(T):
            for part in range(2):
                r = 2 * ROWS * part + t * 32
                SB0[half * T + t, part * 32:part * 32 + 32, :] = (
                    ACC[r:r + 32, lanes] + ACC[r + ROWS:r + ROWS + 32, lanes])
    rs_start(2)

    def rs_sum(it, total):
        def step(d, total):
            gf = g_at(d)
            rs_copy(it, gf, gf).wait_recv()
            return total + (RB0[gf] if it == 2 else RB[it, gf])
        return lax.fori_loop(1, NG, step, total)

    both = rs_sum(2, SB0[g])
    crhs = both[0:32]
    cmat = both[32:64] + damping
    cz = crhs / cmat
    CV[0] = crhs
    CV[1] = cmat
    CV[2] = cz
    G[0:1, :] += fold(crhs * cz)
    G[1:2, :] += fold(cz * cz)

    def ag_copy(it, gt, gf):
        return pltpu.make_async_remote_copy(
            VB.at[it, gf], VB.at[it, gf], ag_s.at[it, gt], ag_r.at[it, gf],
            device_id=(gt, tt), device_id_type=MESH)

    def gather_all(it, v):
        VB[it, g] = v

        @pl.loop(1, NG)
        def _(d):
            ag_copy(it, g_at(d), g).start()

        @pl.loop(1, NG)
        def _(d):
            ag_copy(it, g_at(d), g_at(d)).wait_recv()

        for half in range(2):
            lanes = slice(half * 128, half * 128 + 128)
            for t in range(T):
                hi, lo = split(VB[it, half * T + t])
                TV[t * 32:t * 32 + 32, lanes] = hi.astype(BF16)
                TV[ROWS + t * 32:ROWS + t * 32 + 32, lanes] = lo.astype(BF16)

    def x_copy(it, zs):
        pair = pl.ds(2 * zs, 2)
        return pltpu.make_async_remote_copy(
            XS.at[it, pair], XR.at[it, pair], x_s.at[it, zs], x_r.at[it, zs],
            device_id=partner, device_id_type=MESH)

    def cam_terms(it):
        @pl.loop(0, NG)
        def _(k):
            zs = z_at(k)
            got = jnp.dot(TV[...], OHC[:, block(zs)], preferred_element_type=F32)
            pltpu.make_async_copy(PTR.at[it, zs], PTR.at[it, zs], pt_r.at[it, zs]).wait()
            for core in range(2):
                cols = slice(core * SLOT, core * SLOT + SLOT)
                am = jnp.broadcast_to(AROW[:, half_block(zs, core)], (32, SLOT)) - pat
                acc = jnp.zeros((32, SLOT), F32)
                for t in range(T):
                    acc = jnp.where(
                        am == float(3 * t),
                        got[t * 32:t * 32 + 32, cols]
                        + got[ROWS + t * 32:ROWS + t * 32 + 32, cols], acc)
                v8 = acc[0:8] + acc[8:16] + acc[16:24]
                v1 = jnp.sum(acc[24:32], axis=0, keepdims=True)
                J0, J1, j0, j1 = jac(core, zs)
                mine = jnp.where(c == core, 1.0, 0.0)
                XS[it, 2 * zs + core, :, 0:SLOT] = (
                    jnp.sum(J0 * v8, axis=0, keepdims=True) + j0 * v1
                    + mine * PTR[it, zs, :, 0:SLOT])
                XS[it, 2 * zs + core, :, SLOT:2 * SLOT] = (
                    jnp.sum(J1 * v8, axis=0, keepdims=True) + j1 * v1
                    + mine * PTR[it, zs, :, SLOT:2 * SLOT])
            x_copy(it, zs).start()

    def e_copy(it, zt, zf):
        return pltpu.make_async_remote_copy(
            ER.at[it, 2 * zt + c], EB.at[it, zf], e_s.at[it, zt], e_r.at[it, zf],
            device_id=(g, 2 * zt + c), device_id_type=MESH)

    def cam_scatter(it):
        ACC[0:2 * ROWS, :] = jnp.zeros((2 * ROWS, 256), F32)

        @pl.loop(0, NG)
        def _(k):
            zs = z_at(k)
            x_copy(it, zs).wait_recv()
            for core in range(2):
                e = XS[it, 2 * zs + core] + XR[it, 2 * zs + core]
                ER[it, 2 * zs + core] = e
                e0, e1 = e[:, 0:SLOT], e[:, SLOT:2 * SLOT]
                J0, J1, j0, j1 = jac(core, zs)
                am = jnp.broadcast_to(AROW[:, half_block(zs, core)], (32, SLOT)) - pat
                cam_lhs(0, core * SLOT, J0 * e0 + J1 * e1, j0 * e0 + j1 * e1, am)

            @pl.when(zs != z)
            def _():
                e_copy(it, zs, z).start()

            @pl.when(zs == z)
            def _():
                pltpu.make_async_copy(ER.at[it, 2 * zs + c], EB.at[it, z], e_r.at[it, z]).start()

            mine = ER[it, 2 * zs + c]
            if it == 0:
                G[2:3, :] += fold(mine * mine)
            else:
                before = ER[0, 2 * zs + c]
                G[6:7, :] += fold(mine * before)
                G[7:8, :] += fold(mine * mine)
            ACC[0:2 * ROWS, :] += lax.dot_general(
                LHS[0:2 * ROWS, :], OHC[:, block(zs)], nt, preferred_element_type=F32)

        for half in range(2):
            lanes = slice(half * 128, half * 128 + 128)
            for t in range(T):
                SB[it, half * T + t] = (
                    ACC[t * 32:t * 32 + 32, lanes]
                    + ACC[ROWS + t * 32:ROWS + t * 32 + 32, lanes])
        rs_start(it)

    def point_scatter(it):
        @pl.loop(0, NG)
        def _(k):
            h = z_at(k)
            cols = pl.ds(pl.multiple_of(h * SLOT, SLOT), SLOT)
            pltpu.make_async_copy(EB.at[it, h], EB.at[it, h], e_r.at[it, h]).wait()
            e0, e1 = EB[it, h, :, 0:SLOT], EB[it, h, :, SLOT:2 * SLOT]
            hi, lo = split(jp[0:3, cols] * e0 + jp[3:6, cols] * e1)
            v = jnp.concatenate([hi, lo, jnp.zeros((2, SLOT), F32)], axis=0)
            point_lhs(0, cols, v, APROW[:, cols])

        point_sum(0)
        return PV[0:3, :] + PV[3:6, :]

    gather_all(0, cz)
    cam_terms(0)
    cam_scatter(0)
    pq = point_scatter(0) + damping * PVEC[2]
    pw = pq / PVEC[1]
    PVEC[3] = pq
    PVEC[4] = pw
    point_gather(4, 1)
    G[3:4, :] += fold(pq * pw)
    G[4:5, :] += fold(PVEC[2] * pw)
    G[5:6, :] += fold(pw * pw)

    cq = rs_sum(0, SB[0, g]) + damping * CV[2]
    cw = cq / CV[1]
    CV[3] = cq
    CV[4] = cw
    G[3:4, :] += fold(cq * cw)
    G[4:5, :] += fold(CV[2] * cw)
    G[5:6, :] += fold(cw * cw)
    gather_all(1, cw)
    cam_terms(1)
    cam_scatter(1)

    def gz_copy(zt, zf):
        return pltpu.make_async_remote_copy(
            G, GZ.at[zf], gz_s.at[zt], gz_r.at[zf],
            device_id=(g, 2 * zt + c), device_id_type=MESH)

    def gp_copy(gt, gf):
        return pltpu.make_async_remote_copy(
            GP.at[gf], GP.at[gf], gp_s.at[gt], gp_r.at[gf],
            device_id=(gt, tt), device_id_type=MESH)

    @pl.loop(1, NG)
    def _(k):
        gz_copy(z_at(k), z).start()

    def gz_step(k, total):
        zs = z_at(k)
        gz_copy(zs, zs).wait_recv()
        return total + GZ[zs]

    gsum = lax.fori_loop(1, NG, gz_step, G[...])
    GP[g] = gsum

    @pl.loop(1, NG)
    def _(d):
        gp_copy(g_at(d), g).start()

    PVEC[5] = point_scatter(1) + damping * PVEC[4]

    def gp_step(d, total):
        gf = g_at(d)
        gp_copy(gf, gf).wait_recv()
        return total + GP[gf]

    GZ[z] = lax.fori_loop(1, NG, gp_step, gsum)
    last = pltpu.make_async_remote_copy(
        GZ.at[z], GP.at[NG], gq_s, gq_r, device_id=partner, device_id_type=MESH)
    last.start()
    last.wait_recv()
    sums = jnp.sum(GZ[z] + GP[NG], axis=1, keepdims=True)
    n0, zz, ee, qw, zw, ww, eu, uu = (sums[i:i + 1, :] for i in range(8))
    alpha0 = n0 / (damping * zz + ee)
    n1 = alpha0 * alpha0 * qw - n0
    grow = 1.0 + n1 / n0
    curve1 = (grow * grow * (damping * zz + ee) - 2.0 * grow * alpha0 * (damping * zw + eu)
              + alpha0 * alpha0 * (damping * ww + uu))
    alpha1 = n1 / curve1
    xz = alpha0 + alpha1 * grow
    xw = alpha1 * alpha0

    cv = rs_sum(1, SB[1, g]) + damping * CV[4]
    XF[0] = xz * CV[2] - xw * CV[4]
    XF[1] = CV[0] - xz * CV[3] + xw * cv

    perm = pltpu.make_async_remote_copy(
        XF, XG, pm_s, pm_r, device_id=(z, 2 * g + c), device_id_type=MESH)

    @pl.when(g != z)
    def _():
        perm.start()

    @pl.when(g == z)
    def _():
        pltpu.make_async_copy(XF, XG, pm_r).start()

    xp[...] = xz * PVEC[2] - xw * PVEC[4]
    rp[...] = PVEC[0] - xz * PVEC[3] + xw * PVEC[5]

    @pl.loop(1, NG)
    def _(d):
        zt = z_at(d)
        gt = g_at(d)
        a2a_copy(zt, zt).wait_send()
        gz_copy(zt, zt).wait_send()
        for it in range(2):
            pt_copy(it, zt, zt).wait_send()
            e_copy(it, zt, zt).wait_send()
            ag_copy(it, gt, gt).wait_send()
        for it in range(3):
            rs_copy(it, gt, gt).wait_send()
        gp_copy(gt, gt).wait_send()

    @pl.loop(0, NG)
    def _(zs):
        fwd_copy(c, zs).wait_send()
        for it in range(2):
            x_copy(it, zs).wait_send()

    last.wait_send()

    @pl.when(g != z)
    def _():
        perm.wait_send()

    pltpu.make_async_copy(XG, XG, pm_r).wait()
    for ref, i in ((xc, 0), (rc, 1)):
        for j in range(3):
            ref[0:8, j * 128:(j + 1) * 128] = XG[i, j * 8:j * 8 + 8, :]
            ref[8:9, j * 128:(j + 1) * 128] = XG[i, 24 + j:25 + j, :]


def shards(jac_point, jac_cam, resid, point_index, cam_index):
    NG = lax.axis_size("grp")
    OBS = jac_point.shape[1]
    NPTS = P_DEV
    T = NG // 2
    ROWS = T * 32
    NA = NPTS // 256
    vm = pltpu.VMEM
    dma = pltpu.SemaphoreType.DMA
    scratch = [
        vm((NG, 21, SLOT), F32), vm((2, NG, 21, SLOT), F32),
        vm((256, 2 * OBS), BF16), vm((256, OBS), BF16),
        vm((4 * ROWS, 2 * SLOT), BF16), vm((2 * NA * 8, OBS), BF16),
        vm((4 * ROWS, 256), F32), vm((1, 2 * OBS), F32), vm((1, OBS), F32),
        vm((2 * ROWS, 256), BF16), vm((NA * 8, 256), BF16),
        vm((NG, 64, 128), F32), vm((NG, 64, 128), F32),
        vm((2, NG, 32, 128), F32), vm((2, NG, 32, 128), F32),
        vm((2, NG, 32, 128), F32), vm((5, 32, 128), F32),
        vm((8, NPTS), F32), vm((6, 3, NPTS), F32),
        vm((2, NG, 1, 2 * SLOT), F32), vm((2, NG, 1, 2 * SLOT), F32),
        vm((2, 2 * NG, 1, 2 * SLOT), F32), vm((2, 2 * NG, 1, 2 * SLOT), F32),
        vm((2, 2 * NG, 1, 2 * SLOT), F32), vm((2, NG, 1, 2 * SLOT), F32),
        vm((8, 128), F32), vm((NG, 8, 128), F32), vm((NG + 1, 8, 128), F32),
        vm((2, 32, 128), F32), vm((2, 32, 128), F32),
        dma, dma((NG,)), dma((NG,)), dma((NG,)), dma((NG,)),
        dma((3, NG)), dma((3, NG)), dma((2, NG)), dma((2, NG)),
        dma((2, NG)), dma((2, NG)), dma((2, NG)), dma((2, NG)),
        dma((2, NG)), dma((2, NG)),
        dma((NG,)), dma((NG,)), dma((NG,)), dma((NG,)), dma, dma, dma, dma,
    ]
    outs = ((3, NPTS), (9, CAM_DEV), (3, NPTS), (9, CAM_DEV))
    return pl.pallas_call(
        functools.partial(kernel, NG, OBS, NPTS),
        name="cg",
        out_shape=tuple(jax.ShapeDtypeStruct(s, F32) for s in outs),
        in_specs=[pl.BlockSpec(memory_space=pltpu.VMEM)] * 5,
        out_specs=tuple(pl.BlockSpec(memory_space=pltpu.VMEM) for _ in outs),
        scratch_shapes=scratch,
        compiler_params=pltpu.CompilerParams(
            collective_id=0, has_side_effects=True, vmem_limit_bytes=48 << 20),
    )(jac_point, jac_cam, resid, point_index.reshape(1, OBS), cam_index.reshape(1, OBS))


P_DEV = 4096


def solution(mesh):
    cols, flat = P(None, ("grp", "tile")), P(("grp", "tile"))
    return jax.shard_map(
        shards, mesh=mesh, in_specs=(cols, cols, cols, flat, flat),
        out_specs=(cols,) * 4, check_vma=False)
```

time: 1100 us -> 129 us (0.12)
  the two profiles are of different devices: /device:TPU:1 before, /device:TPU:31 now
where the time goes in v1:
time: 129 us
  Pallas kernels  122 us (95%)
  local copies, waits for them, and re-layouts  6.56 us (5%)
    pallas_call x1, Pallas kernels, shards(): pl.pallas_call(functools.partial(kernel, NG, OBS, NPTS), name='cg', out_s...  122 us
    unnamed x14, local copies, waits for them, and re-layouts  6.56 us

profile of v1, /device:TPU:31, one launch (start us, length us, event | category | flops | bytes accessed | tf_op | source)
XLA Modules:
  0.0 128.8 jit_solution(11264207892289780454)
XLA Ops:
  0.6 0.0 copy-start
  0.6 1.0 copy-done
  1.6 0.0 copy-start.1
  1.6 0.9 copy-done.1
  2.5 0.0 copy-start.2
  2.5 0.8 copy-done.2
  3.3 0.0 copy-start.3
  3.3 0.7 copy-done.3
  4.0 0.0 copy-start.4
  4.0 0.7 copy-done.4
  4.7 121.6 %cg.1 = (f32[3,4096]{1,0:T(4,128)S(1)}, f32[9,384]{1,0:T(8,128)S(1)}, f32[3,4096]{1,0:T(4,128)S(1)}, f32[9,384]{1,0:T(8,128)S(1)}) custom-call(f32[6,4096]{1,0:T(8,128)S(1)} %copy-done.1, f32[18,4096]{1,0:T(8,128)S(1)} %copy-done, f32[2,4096]{1,0:T(2,128)S(1)} %copy-done.2, s32[1,4096]{1,0:T(1,128)S(1)} %bitcast.2, s32[1,4096]{1,0:T(1,128)S(1)} %bitcast.3), custom_call_target="tpu_custom_call" | custom-call | tf_op jit(solution)/shard_map/cg/pallas_call | solution.py:558
  126.3 0.6 copy.13
  126.9 0.6 copy.14
  127.5 0.6 copy.15
  128.2 0.6 copy.16
Async XLA Ops:
  0.6 1.0 copy-start
  1.6 0.9 copy-start.1
  2.5 0.8 copy-start.2
  3.3 0.7 copy-start.3
  4.0 0.7 copy-start.4

commit v2 on v1

v2 whole, which is shorter than its diff:
```python
import functools

import jax
import jax.numpy as jnp
from jax import lax
from jax.experimental import pallas as pl
from jax.experimental.pallas import tpu as pltpu
from jax.sharding import PartitionSpec as P

F32, BF16, I32 = jnp.float32, jnp.bfloat16, jnp.int32
MESH = pl.DeviceIdType.MESH
SLOT = 256
CAM_DEV = 384
damping = 1.0


class Marks:
    def __init__(self):
        self.scope = None

    def __call__(self, name):
        if self.scope is not None:
            self.scope.__exit__(None, None, None)
        self.scope = None
        if name:
            self.scope = jax.named_scope(name)
            self.scope.__enter__()


def spread(n, d):
    half = lax.div(d + 1, jnp.int32(2))
    return half * (2 * lax.rem(d, jnp.int32(2)) - 1) + n


def kernel(
    NG, OBS, NPTS,
    jp_in, jc_in, res_in, pidx_in, cidx_in,
    xp_out, xc_out, rp_out, rc_out,
    jp, jc, res, pidx, cidx, in_s,
    S, R2, OHC, OHP, OHI, LHSI, LHS, LHSP, ACC, AROW, APROW, TV, TP,
    SB0, RB0, SB, RB, VB, CV, PV, PVEC,
    PTS, PTR, XS, XR, ER, EB, G, GS, GZ, GP, XE, XEG, XQ, XQG, XV, XG,
    loc, a2a_s, a2a_r, fwd_s, fwd_r, rs_s, rs_r, ag_s, ag_r,
    pt_s, pt_r, x_s, x_r, e_s, e_r, gz_s, gz_r, gp_s, gp_r, gq_s, gq_r, pe_s, pe_r, xp, xc, rp, rc, out_s,
):
    mark = Marks()
    moves = [pltpu.make_async_copy(a, b, in_s.at[i]) for i, (a, b) in enumerate((
        (jc_in, jc), (res_in, res), (cidx_in, cidx), (jp_in, jp), (pidx_in, pidx)))]
    for m in moves:
        m.start()
    QB = min(BLOCKS, NG)
    T = NG // 2
    ROWS = T * 32
    NA = NPTS // 256
    ng = jnp.int32(NG)
    g = lax.axis_index("grp")
    tt = lax.axis_index("tile")
    z = lax.div(tt, jnp.int32(2))
    c = lax.rem(tt, jnp.int32(2))
    partner = (g, 2 * z + 1 - c)

    two = jnp.int32(2)

    def z_at(k):
        k = jnp.int32(k)
        if NG == 16:
            far = 2 * (8 - lax.div(k - 4, two)) - 1 + jnp.where(k > 5, lax.rem(k, two), 0)
            k = jnp.where(k <= 4, k, far)
        return lax.rem(z + spread(ng, k), ng)

    def g_at(d):
        return lax.rem(g + d, ng)

    four = jnp.int32(4)

    def owner(h, k):
        d = lax.rem(k - h + ng, ng)
        if NG != 16:
            return lax.rem(h + d, ng)
        y = lax.rem(lax.div(h, four) + lax.div(d + 2, four) + 2, four)
        return 4 * y + lax.rem(h + d, four)

    def chunk_of(gg, h):
        if NG != 16:
            return gg
        y = lax.div(gg, four) - lax.div(h, four) + 4
        x = lax.rem(lax.rem(gg, four) - lax.rem(h, four) + 4, four)
        a = lax.rem(y + 2 - lax.div(x, jnp.int32(2)) + 4, four)
        return lax.rem(h + 4 * a + x, ng)

    mine_k = chunk_of(g, z)
    final = (z, 2 * mine_k + c)
    stays = jnp.logical_and(g == z, mine_k == z)

    mark("signal")
    bar = pltpu.get_barrier_semaphore()

    @pl.loop(1, NG)
    def _(d):
        pl.semaphore_signal(bar, inc=1, device_id=(g, 2 * z_at(d) + c), device_id_type=MESH)
        pl.semaphore_signal(bar, inc=1, device_id=(g_at(d), tt), device_id_type=MESH)

    pl.semaphore_signal(bar, inc=1, device_id=partner, device_id_type=MESH)

    @pl.when(jnp.logical_not(stays))
    def _():
        pl.semaphore_signal(bar, inc=1, device_id=(owner(g, z), 2 * g + c), device_id_type=MESH)

    mark("pack")
    for m in moves[:3]:
        m.wait()

    @pl.loop(0, NG)
    def _(h):
        cols = pl.ds(pl.multiple_of(h * SLOT, SLOT), SLOT)
        S[h, 0:8, :] = jc[0:8, cols]
        S[h, 8:16, :] = jc[9:17, cols]
        S[h, 16:17, :] = jc[8:9, cols]
        S[h, 17:18, :] = jc[17:18, cols]
        S[h, 18:20, :] = res[:, cols]
        S[h, 20:21, :] = cidx[:, cols].astype(F32)

    G[...] = jnp.zeros_like(G)

    mark("barrier")
    pl.semaphore_wait(bar, 2 * (NG - 1) + 1 + jnp.where(stays, 0, 1))

    def a2a_copy(zt, zf):
        return pltpu.make_async_remote_copy(
            S.at[zt], R2.at[c, zf], a2a_s.at[zt], a2a_r.at[zf],
            device_id=(g, 2 * zt + c), device_id_type=MESH)

    mark("a2a_start")
    own = pltpu.make_async_copy(S.at[z], R2.at[c, z], loc)
    own.start()

    @pl.loop(1, NG)
    def _(k):
        a2a_copy(z_at(k), z).start()

    def fold(v):
        out = v[:, 0:128]
        for i in range(1, v.shape[1] // 128):
            out = out + v[:, i * 128:(i + 1) * 128]
        return jnp.sum(out, axis=0, keepdims=True)

    def point_lhs(row0, cols, v, ap):
        v2 = jnp.concatenate([v, v], axis=0)
        low = lax.broadcasted_iota(I32, (16, SLOT), 0) < 8
        am = jnp.broadcast_to(ap, (16, SLOT)) - jnp.where(low, 0.0, 1.0)
        for i in range(NA // 2):
            LHSP[row0 + i * 16:row0 + i * 16 + 16, cols] = jnp.where(
                am == float(2 * i), v2, 0.0).astype(BF16)

    def split(v):
        hi = v.astype(BF16).astype(F32)
        return hi, v - hi

    nt = (((1,), (1,)), ((), ()))

    def point_sum(row0):
        out = lax.dot_general(LHSP[row0:row0 + NA * 8, :], OHP[...], nt,
                              preferred_element_type=F32)
        for a in range(NA):
            PV[:, a * 256:(a + 1) * 256] = out[a * 8:(a + 1) * 8, :]

    def point_gather(src, it):
        for i in range(NA // 2):
            parts = []
            for a in (2 * i, 2 * i + 1):
                hi, lo = split(PVEC[src, :, a * 256:(a + 1) * 256])
                parts += [hi, lo, jnp.zeros((2, 256), F32)]
            TP[i * 16:i * 16 + 16, :] = jnp.concatenate(parts, axis=0).astype(BF16)

        @pl.loop(0, NG // QB)
        def _(i):
            cols = pl.ds(pl.multiple_of(i * (QB * SLOT), QB * SLOT), QB * SLOT)
            got = jnp.dot(TP[...], OHP[:, cols], preferred_element_type=F32)
            ap = jnp.broadcast_to(APROW[:, cols], (8, QB * SLOT))
            acc = jnp.zeros((8, QB * SLOT), F32)
            for a in range(NA):
                acc = jnp.where(ap == float(a), got[a * 8:(a + 1) * 8, :], acc)
            v = acc[0:3] + acc[3:6]
            t0 = jnp.sum(jp[0:3, cols] * v, axis=0, keepdims=True)
            t1 = jnp.sum(jp[3:6, cols] * v, axis=0, keepdims=True)
            for b in range(QB):
                PTS[it, i * QB + b, :, 0:SLOT] = t0[:, b * SLOT:(b + 1) * SLOT]
                PTS[it, i * QB + b, :, SLOT:2 * SLOT] = t1[:, b * SLOT:(b + 1) * SLOT]

        pltpu.make_async_copy(PTS.at[it, z], PTR.at[it, z], pt_r.at[it, z]).start()

        @pl.loop(1, NG)
        def _(k):
            pt_copy(it, z_at(k), z).start()

    def pt_copy(it, zt, zf):
        return pltpu.make_async_remote_copy(
            PTS.at[it, zt], PTR.at[it, zf], pt_s.at[it, zt], pt_r.at[it, zf],
            device_id=(g, 2 * zt + c), device_id_type=MESH)

    mark("pt_init")
    for m in moves[3:]:
        m.wait()

    @pl.loop(0, NG)
    def _(h):
        cols = pl.ds(pl.multiple_of(h * SLOT, SLOT), SLOT)
        p = pidx[:, cols]
        ap = lax.shift_right_logical(p, 8).astype(F32)
        n = (p & 255).astype(F32)
        APROW[:, cols] = ap
        row = lax.broadcasted_iota(I32, (256, SLOT), 0).astype(F32)
        OHP[:, cols] = jnp.where(row == jnp.broadcast_to(n, (256, SLOT)), 1.0, 0.0).astype(BF16)
        j0, j1 = jp[0:3, cols], jp[3:6, cols]
        s0, s1 = res[0:1, cols], res[1:2, cols]
        v = jnp.concatenate(
            [-(j0 * s0 + j1 * s1), j0 * j0 + j1 * j1, jnp.zeros((2, SLOT), F32)], axis=0)
        hi, lo = split(v)
        point_lhs(0, cols, hi, ap)
        point_lhs(NA * 8, cols, lo, ap)

    mark("pt_dot")
    out = lax.dot_general(LHSP[...], OHP[...], nt, preferred_element_type=F32)
    for a in range(NA):
        PV[:, a * 256:(a + 1) * 256] = (
            out[a * 8:(a + 1) * 8, :] + out[(NA + a) * 8:(NA + a + 1) * 8, :])
    prhs = PV[0:3, :]
    pmat = PV[3:6, :] + damping
    pz = prhs / pmat
    PVEC[0] = prhs
    PVEC[1] = pmat
    PVEC[2] = pz
    G[0:1, :] += fold(prhs * pz)
    G[1:2, :] += fold(pz * pz)
    mark("pt_gather0")
    point_gather(2, 0)

    pat_row = lax.broadcasted_iota(I32, (32, SLOT), 0)
    pat = jnp.where(pat_row < 8, 0, jnp.where(
        pat_row < 16, 1, jnp.where(
            pat_row < 24, 2, jnp.where(pat_row < 27, pat_row - 24, 2000)))).astype(F32)

    def cam_lhs(ref, row0, col0, v8, v1, am, t0, nt_):
        h8, l8 = split(v8)
        h1, l1 = split(v1)
        h1 = jnp.broadcast_to(h1, (8, SLOT))
        l1 = jnp.broadcast_to(l1, (8, SLOT))
        hi = jnp.concatenate([h8, h8, h8, h1], axis=0)
        lo = jnp.concatenate([l8, l8, l8, l1], axis=0)
        for t in range(nt_):
            hit = am == float(3 * (t0 + t))
            ref[row0 + t * 32:row0 + t * 32 + 32, col0:col0 + SLOT] = (
                jnp.where(hit, hi, 0.0).astype(BF16))
            ref[row0 + nt_ * 32 + t * 32:row0 + nt_ * 32 + t * 32 + 32, col0:col0 + SLOT] = (
                jnp.where(hit, lo, 0.0).astype(BF16))

    def jac(core, zs):
        return (R2[core, zs, 0:8, :], R2[core, zs, 8:16, :],
                R2[core, zs, 16:17, :], R2[core, zs, 17:18, :])

    def block(zs):
        return pl.ds(pl.multiple_of(zs * (2 * SLOT), 2 * SLOT), 2 * SLOT)

    def half_block(zs, core):
        return pl.ds(pl.multiple_of(zs * (2 * SLOT) + core * SLOT, SLOT), SLOT)

    def fwd_copy(core, zs):
        return pltpu.make_async_remote_copy(
            R2.at[core, zs], R2.at[core, zs], fwd_s.at[zs], fwd_r.at[zs],
            device_id=partner, device_id_type=MESH)

    mark("cam_init")
    ACC[...] = jnp.zeros_like(ACC)
    own.wait()
    fwd_copy(c, z).start()
    log_t = T.bit_length() - 1

    def arrived(k):
        zn = z_at(k)
        a2a_copy(zn, zn).wait_recv()
        fwd_copy(c, zn).start()

    arrived(1)

    @pl.loop(0, NG // 2)
    def _(k):
        @pl.when(2 * k + 2 < NG)
        def _():
            arrived(2 * k + 2)
            arrived(2 * k + 3)

        tot = None
        for b in range(2):
            zs = z_at(2 * k + b)
            fwd_copy(1 - c, zs).wait_recv()
        for b in range(2):
            zs = z_at(2 * k + b)
            for core in range(2):
                idx = R2[core, zs, 20:21, :].astype(I32)
                q = lax.shift_right_logical(idx, 7)
                t = lax.shift_right_logical(q * 171, 9)
                tau = lax.shift_right_logical(t, 1)
                a = 3 * (tau & (T - 1)) + (q - 3 * t)
                a = jnp.where((t & 1) == c, a, -1000).astype(F32)
                n = (lax.shift_right_logical(tau, log_t) * 128 + (idx & 127)).astype(F32)
                AROW[:, half_block(zs, core)] = a
                row = lax.broadcasted_iota(I32, (256, SLOT), 0).astype(F32)
                oh = jnp.where(row == jnp.broadcast_to(n, (256, SLOT)), 1.0, 0.0).astype(BF16)
                OHC[:, half_block(zs, core)] = oh
                col = (2 * b + core) * SLOT
                OHI[:, col:col + SLOT] = oh
                am = jnp.broadcast_to(a, (32, SLOT)) - pat
                J0, J1, j0, j1 = jac(core, zs)
                s0, s1 = R2[core, zs, 18:19, :], R2[core, zs, 19:20, :]
                cam_lhs(LHSI, 0, col, -(J0 * s0 + J1 * s1), -(j0 * s0 + j1 * s1), am, 0, T)
                cam_lhs(LHSI, 2 * ROWS, col, J0 * J0 + J1 * J1, j0 * j0 + j1 * j1, am, 0, T)
        ACC[...] += lax.dot_general(LHSI[...], OHI[...], nt, preferred_element_type=F32)

    def rs_copy(it, gt, gf, k=0):
        if it == 2:
            src, dst = SB0.at[k], RB0.at[gf]
        else:
            src, dst = SB.at[it, k], RB.at[it, gf]
        return pltpu.make_async_remote_copy(
            src, dst, rs_s.at[it, gt], rs_r.at[it, gf],
            device_id=(gt, tt), device_id_type=MESH)

    def rs_send(it, k):
        gt = owner(z, k)

        @pl.when(gt != g)
        def _():
            rs_copy(it, gt, g, k).start()

    mark("rs_init_send")
    for half in range(2):
        lanes = slice(half * 128, half * 128 + 128)
        for t in range(T):
            for part in range(2):
                r = 2 * ROWS * part + t * 32
                SB0[half * T + t, part] = (
                    ACC[r:r + 27, lanes] + ACC[r + ROWS:r + ROWS + 27, lanes])

    @pl.loop(1, NG)
    def _(d):
        rs_send(2, chunk_of(g_at(d), z))


    def rs_sum(it, total):
        def step(d, total):
            gf = g_at(d)
            rs_copy(it, gf, gf).wait_recv()
            return total + (RB0[gf] if it == 2 else RB[it, gf])
        return lax.fori_loop(1, NG, step, total)

    mark("rs_init_wait")
    both = rs_sum(2, SB0[mine_k])
    crhs = both[0]
    cmat = both[1] + damping
    cz = crhs / cmat
    CV[0] = crhs
    CV[1] = cmat
    CV[2] = cz
    G[0:1, :] += fold(crhs * cz)
    G[1:2, :] += fold(cz * cz)

    def ag_copy(it, gt, gf):
        k = chunk_of(gf, z)
        return pltpu.make_async_remote_copy(
            VB.at[it, k], VB.at[it, k], ag_s.at[it, gt], ag_r.at[it, gf],
            device_id=(gt, tt), device_id_type=MESH)

    def gather_all(it, v):
        VB[it, mine_k] = v

        @pl.loop(1, NG)
        def _(d):
            ag_copy(it, g_at(d), g).start()

        @pl.loop(1, NG)
        def _(d):
            ag_copy(it, g_at(d), g_at(d)).wait_recv()

        for half in range(2):
            lanes = slice(half * 128, half * 128 + 128)
            for t in range(T):
                hi, lo = split(jnp.concatenate(
                    [VB[it, half * T + t], jnp.zeros((5, 128), F32)], axis=0))
                TV[t * 32:t * 32 + 32, lanes] = hi.astype(BF16)
                TV[ROWS + t * 32:ROWS + t * 32 + 32, lanes] = lo.astype(BF16)

    QW = 2 * SLOT * QB

    NC = NG // QB

    def far_first(i):
        if NC == 1:
            return i
        off = jnp.where(i == 0, 2, jnp.where(i == 1, 1, jnp.where(i == 2, 3, 0)))
        return lax.rem(lax.div(z, jnp.int32(QB)) + off, jnp.int32(NC))

    def chunk(i):
        return pl.ds(pl.multiple_of(i * QW, QW), QW)

    def x_copy(it, i):
        rows = pl.ds(2 * QB * i, 2 * QB)
        return pltpu.make_async_remote_copy(
            XS.at[it, rows], XR.at[it, rows], x_s.at[it, i], x_r.at[it, i],
            device_id=partner, device_id_type=MESH)

    def e_copy(it, zt, zf):
        return pltpu.make_async_remote_copy(
            ER.at[it, 2 * zt + c], EB.at[it, zf], e_s.at[it, zt], e_r.at[it, zf],
            device_id=(g, 2 * zt + c), device_id_type=MESH)

    def cam_errors(it):
        @pl.loop(0, NG)
        def _(zs):
            pltpu.make_async_copy(PTR.at[it, zs], PTR.at[it, zs], pt_r.at[it, zs]).wait()

        @pl.loop(0, NC)
        def _(k):
            i = far_first(k)
            got = jnp.dot(TV[...], OHC[:, chunk(i)], preferred_element_type=F32)
            for b in range(2 * QB):
                zs, core = i * QB + b // 2, b % 2
                cols = slice(b * SLOT, b * SLOT + SLOT)
                am = jnp.broadcast_to(AROW[:, half_block(zs, core)], (32, SLOT)) - pat
                acc = jnp.zeros((32, SLOT), F32)
                for t in range(T):
                    acc = jnp.where(
                        am == float(3 * t),
                        got[t * 32:t * 32 + 32, cols]
                        + got[ROWS + t * 32:ROWS + t * 32 + 32, cols], acc)
                v8 = acc[0:8] + acc[8:16] + acc[16:24]
                J0, J1, j0, j1 = jac(core, zs)
                mine = jnp.where(c == core, 1.0, 0.0)
                XS[it, 2 * zs + core, :, 0:SLOT] = (
                    jnp.sum(J0 * v8 + j0 * acc[24:32], axis=0, keepdims=True)
                    + mine * PTR[it, zs, :, 0:SLOT])
                XS[it, 2 * zs + core, :, SLOT:2 * SLOT] = (
                    jnp.sum(J1 * v8 + j1 * acc[24:32], axis=0, keepdims=True)
                    + mine * PTR[it, zs, :, SLOT:2 * SLOT])
            x_copy(it, i).start()

            @pl.when(k > 0)
            def _():
                errors_of(it, far_first(k - 1))
                errors_send(it, far_first(k - 1))

        mark("err")
        errors_of(it, far_first(jnp.int32(NC - 1)))

    def errors_of(it, i):
        x_copy(it, i).wait_recv()
        for b in range(2 * QB):
            row = 2 * QB * i + b
            ER[it, row] = XS[it, row] + XR[it, row]
        for b in range(QB):
            mine = ER[it, 2 * (i * QB + b) + c]
            if it == 0:
                G[2:3, :] += fold(mine * mine)
            else:
                before = ER[0, 2 * (i * QB + b) + c]
                G[6:7, :] += fold(mine * before)
                G[7:8, :] += fold(mine * mine)

    def errors_send(it, i):
        @pl.loop(0, QB)
        def _(b):
            zs = i * QB + b

            @pl.when(zs != z)
            def _():
                e_copy(it, zs, z).start()

            @pl.when(zs == z)
            def _():
                pltpu.make_async_copy(ER.at[it, 2 * z + c], EB.at[it, z], e_r.at[it, z]).start()

    NP = 2 if T > 1 else 1
    TH = T // NP
    RH = TH * 32
    WS = min(2 * QW, 2 * OBS)

    def cam_scatter(it):
        for part in range(NP):
            ACC[0:2 * RH, :] = jnp.zeros((2 * RH, 256), F32)

            @pl.loop(0, 2 * OBS // WS)
            def _(i):
                for b in range(WS // SLOT):
                    zs, core = i * (WS // (2 * SLOT)) + b // 2, b % 2
                    e0 = ER[it, 2 * zs + core, :, 0:SLOT]
                    e1 = ER[it, 2 * zs + core, :, SLOT:2 * SLOT]
                    J0, J1, j0, j1 = jac(core, zs)
                    am = jnp.broadcast_to(AROW[:, half_block(zs, core)], (32, SLOT)) - pat
                    cam_lhs(LHS, 0, b * SLOT, J0 * e0 + J1 * e1, j0 * e0 + j1 * e1, am,
                            part * TH, TH)
                cols = pl.ds(pl.multiple_of(i * WS, WS), WS)
                ACC[0:2 * RH, :] += lax.dot_general(
                    LHS[...], OHC[:, cols], nt, preferred_element_type=F32)

            for half in range(2):
                lanes = slice(half * 128, half * 128 + 128)
                for t in range(TH):
                    SB[it, half * T + part * TH + t] = (
                        ACC[t * 32:t * 32 + 27, lanes]
                        + ACC[RH + t * 32:RH + t * 32 + 27, lanes])

            @pl.loop(0, 2 * TH)
            def _(d):
                n = lax.rem(g + d, jnp.int32(2 * TH))
                rs_send(it, lax.div(n, jnp.int32(TH)) * T + part * TH + lax.rem(n, jnp.int32(TH)))

    def point_scatter(it):
        @pl.loop(0, NG)
        def _(k):
            h = z_at(k)
            cols = pl.ds(pl.multiple_of(h * SLOT, SLOT), SLOT)
            pltpu.make_async_copy(EB.at[it, h], EB.at[it, h], e_r.at[it, h]).wait()
            e0, e1 = EB[it, h, :, 0:SLOT], EB[it, h, :, SLOT:2 * SLOT]
            hi, lo = split(jp[0:3, cols] * e0 + jp[3:6, cols] * e1)
            v = jnp.concatenate([hi, lo, jnp.zeros((2, SLOT), F32)], axis=0)
            point_lhs(0, cols, v, APROW[:, cols])

        point_sum(0)
        return PV[0:3, :] + PV[3:6, :]

    mark("ag0")
    gather_all(0, cz)
    XE[0] = crhs
    XE[1] = cmat

    def to_final(src, dst, n):
        return pltpu.make_async_remote_copy(
            src, dst, pe_s.at[n], pe_r.at[n], device_id=final, device_id_type=MESH)

    def final_start(src, dst, n):
        @pl.when(jnp.logical_not(stays))
        def _():
            to_final(src, dst, n).start()

        @pl.when(stays)
        def _():
            pltpu.make_async_copy(src, dst, pe_r.at[n]).start()

    final_start(XE, XEG, 0)
    mark("terms0")
    cam_errors(0)
    errors_send(0, far_first(jnp.int32(NC - 1)))

    mark("scat0")
    cam_scatter(0)
    mark("pscat0")
    pq = point_scatter(0) + damping * PVEC[2]
    pw = pq / PVEC[1]
    PVEC[3] = pq
    PVEC[4] = pw
    mark("pt_gather1")
    point_gather(4, 1)
    G[3:4, :] += fold(pq * pw)
    G[4:5, :] += fold(PVEC[2] * pw)
    G[5:6, :] += fold(pw * pw)

    mark("rs0_wait")
    cq = rs_sum(0, SB[0, mine_k]) + damping * CV[2]
    cw = cq / CV[1]
    CV[3] = cq
    CV[4] = cw
    G[3:4, :] += fold(cq * cw)
    G[4:5, :] += fold(CV[2] * cw)
    G[5:6, :] += fold(cw * cw)
    XQ[...] = cq
    mark("ag1")
    gather_all(1, cw)
    final_start(XQ, XQG, 1)
    mark("terms1")
    cam_errors(1)

    def gz_copy(zt, zf):
        return pltpu.make_async_remote_copy(
            GS, GZ.at[zf], gz_s.at[zt], gz_r.at[zf],
            device_id=(g, 2 * zt + c), device_id_type=MESH)

    def gp_copy(gt, gf):
        return pltpu.make_async_remote_copy(
            GP.at[gf], GP.at[gf], gp_s.at[gt], gp_r.at[gf],
            device_id=(gt, tt), device_id_type=MESH)

    lane = lax.broadcasted_iota(I32, (8, 128), 1)
    row8 = lax.broadcasted_iota(I32, (8, 128), 0)
    each = jnp.broadcast_to(jnp.sum(G[...], axis=1, keepdims=True), (8, 128))
    mine = jnp.sum(jnp.where(lane == row8, each, 0.0), axis=0, keepdims=True)
    GS[...] = mine

    @pl.loop(1, NG)
    def _(k):
        gz_copy(z_at(k), z).start()

    errors_send(1, far_first(jnp.int32(NC - 1)))
    mark("scat1")
    cam_scatter(1)
    mark("pscat1")
    PVEC[5] = point_scatter(1) + damping * PVEC[4]
    mark("gram_z")

    def gz_step(k, total):
        zs = z_at(k)
        gz_copy(zs, zs).wait_recv()
        return total + GZ[zs]

    gsum = lax.fori_loop(1, NG, gz_step, mine)
    GP[g] = gsum

    @pl.loop(1, NG)
    def _(d):
        gp_copy(g_at(d), g).start()

    mark("rs1_wait")
    XV[...] = rs_sum(1, SB[1, mine_k]) + damping * CV[4]
    mark("perm")
    final_start(XV, XG, 2)
    mark("gram_p")

    def gp_step(d, total):
        gf = g_at(d)
        gp_copy(gf, gf).wait_recv()
        return total + GP[gf]

    GZ[z] = lax.fori_loop(1, NG, gp_step, gsum)
    last = pltpu.make_async_remote_copy(
        GZ.at[z], GP.at[NG], gq_s, gq_r, device_id=partner, device_id_type=MESH)
    last.start()
    last.wait_recv()
    mark("final")
    total = GZ[z] + GP[NG]
    n0, zz, ee, qw, zw, ww, eu, uu = (total[:, i:i + 1] for i in range(8))
    alpha0 = n0 / (damping * zz + ee)
    n1 = alpha0 * alpha0 * qw - n0
    grow = 1.0 + n1 / n0
    curve1 = (grow * grow * (damping * zz + ee) - 2.0 * grow * alpha0 * (damping * zw + eu)
              + alpha0 * alpha0 * (damping * ww + uu))
    alpha1 = n1 / curve1
    xz = alpha0 + alpha1 * grow
    xw = alpha1 * alpha0

    xp[...] = xz * PVEC[2] - xw * PVEC[4]
    rp[...] = PVEC[0] - xz * PVEC[3] + xw * PVEC[5]
    results = [pltpu.make_async_copy(a, b, out_s.at[i]) for i, (a, b) in enumerate((
        (xp, xp_out), (rp, rp_out), (xc, xc_out), (rc, rc_out)))]
    results[0].start()
    results[1].start()

    def put(ref, v):
        for j in range(3):
            ref[0:8, j * 128:(j + 1) * 128] = v[j * 8:j * 8 + 8, :]
            ref[8:9, j * 128:(j + 1) * 128] = v[24 + j:25 + j, :]

    pltpu.make_async_copy(XEG, XEG, pe_r.at[0]).wait()
    pltpu.make_async_copy(XQG, XQG, pe_r.at[1]).wait()
    put(xc, (xz * XEG[0] - xw * XQG[...]) / XEG[1])
    results[2].start()
    base = XEG[0] - xz * XQG[...]

    mark("sends")
    @pl.loop(1, NG)
    def _(d):
        zt = z_at(d)
        gt = g_at(d)
        a2a_copy(zt, zt).wait_send()
        gz_copy(zt, zt).wait_send()
        for it in range(2):
            pt_copy(it, zt, zt).wait_send()
            e_copy(it, zt, zt).wait_send()
            ag_copy(it, gt, gt).wait_send()
        for it in range(3):
            rs_copy(it, gt, gt).wait_send()
        gp_copy(gt, gt).wait_send()

    @pl.loop(0, NG)
    def _(zs):
        fwd_copy(c, zs).wait_send()

    @pl.loop(0, NG // QB)
    def _(i):
        for it in range(2):
            x_copy(it, i).wait_send()

    last.wait_send()

    @pl.when(jnp.logical_not(stays))
    def _():
        to_final(XE, XEG, 0).wait_send()
        to_final(XQ, XQG, 1).wait_send()
        to_final(XV, XG, 2).wait_send()

    mark("perm_wait")
    pltpu.make_async_copy(XG, XG, pe_r.at[2]).wait()
    put(rc, base + xw * XG[...])
    results[3].start()
    for m in results:
        m.wait()
    mark(None)


def shards(jac_point, jac_cam, resid, point_index, cam_index):
    NG = lax.axis_size("grp")
    OBS = jac_point.shape[1]
    NPTS = P_DEV
    T = NG // 2
    ROWS = T * 32
    NA = NPTS // 256
    vm = pltpu.VMEM
    dma = pltpu.SemaphoreType.DMA
    QB = min(BLOCKS, NG)
    scratch = [
        vm((6, OBS), F32), vm((18, OBS), F32), vm((2, OBS), F32),
        vm((1, OBS), I32), vm((1, OBS), I32), dma((5,)),
        vm((NG, 21, SLOT), F32), vm((2, NG, 21, SLOT), F32),
        vm((256, 2 * OBS), BF16), vm((256, OBS), BF16),
        vm((256, 4 * SLOT), BF16), vm((4 * ROWS, 4 * SLOT), BF16),
        vm((2 * ROWS // min(2, T), min(4 * SLOT * QB, 2 * OBS)), BF16), vm((2 * NA * 8, OBS), BF16),
        vm((4 * ROWS, 256), F32), vm((1, 2 * OBS), F32), vm((1, OBS), F32),
        vm((2 * ROWS, 256), BF16), vm((NA * 8, 256), BF16),
        vm((NG, 2, 27, 128), F32), vm((NG, 2, 27, 128), F32),
        vm((2, NG, 27, 128), F32), vm((2, NG, 27, 128), F32),
        vm((2, NG, 27, 128), F32), vm((5, 27, 128), F32),
        vm((8, NPTS), F32), vm((6, 3, NPTS), F32),
        vm((2, NG, 1, 2 * SLOT), F32), vm((2, NG, 1, 2 * SLOT), F32),
        vm((2, 2 * NG, 1, 2 * SLOT), F32), vm((2, 2 * NG, 1, 2 * SLOT), F32),
        vm((2, 2 * NG, 1, 2 * SLOT), F32), vm((2, NG, 1, 2 * SLOT), F32),
        vm((8, 128), F32), vm((1, 128), F32),
        vm((NG, 1, 128), F32), vm((NG + 1, 1, 128), F32),
        vm((2, 27, 128), F32), vm((2, 27, 128), F32),
        vm((27, 128), F32), vm((27, 128), F32),
        vm((27, 128), F32), vm((27, 128), F32),
        dma, dma((NG,)), dma((NG,)), dma((NG,)), dma((NG,)),
        dma((3, NG)), dma((3, NG)), dma((2, NG)), dma((2, NG)),
        dma((2, NG)), dma((2, NG)), dma((2, NG // QB)), dma((2, NG // QB)),
        dma((2, NG)), dma((2, NG)),
        dma((NG,)), dma((NG,)), dma((NG,)), dma((NG,)), dma, dma, dma((3,)), dma((3,)),
    ]
    outs = ((3, NPTS), (9, CAM_DEV), (3, NPTS), (9, CAM_DEV))
    made = pl.pallas_call(
        functools.partial(kernel, NG, OBS, NPTS),
        name="cg",
        out_shape=tuple(jax.ShapeDtypeStruct(s, F32) for s in outs),
        in_specs=[pl.BlockSpec(memory_space=pltpu.HBM)] * 5,
        out_specs=tuple(pl.BlockSpec(memory_space=pltpu.HBM) for _ in outs),
        scratch_shapes=scratch + [vm(s, F32) for s in outs] + [dma((4,))],
        compiler_params=pltpu.CompilerParams(
            collective_id=0, has_side_effects=True, vmem_limit_bytes=VMEM_ALL),
    )(jac_point, jac_cam, resid, point_index.reshape(1, OBS), cam_index.reshape(1, OBS))
    return pl.pallas_call(
        store,
        name="store",
        out_shape=tuple(jax.ShapeDtypeStruct(s, F32) for s in outs),
        in_specs=[pl.BlockSpec(memory_space=pltpu.HBM)] * 4,
        out_specs=tuple(pl.BlockSpec(memory_space=pltpu.HBM) for _ in outs),
        scratch_shapes=[vm(s, F32) for s in outs] + [dma((4,)), dma((4,))],
        compiler_params=pltpu.CompilerParams(vmem_limit_bytes=VMEM_ALL),
    )(*made)


def store(*refs):
    got, sent = refs[12], refs[13]
    loads = [pltpu.make_async_copy(refs[i], refs[8 + i], got.at[i]) for i in range(4)]
    stores = [pltpu.make_async_copy(refs[8 + i], refs[4 + i], sent.at[i]) for i in range(4)]
    for m in loads:
        m.start()
    for i in range(4):
        loads[i].wait()
        stores[i].start()
    for m in stores:
        m.wait()


P_DEV = 4096
VMEM_ALL = 67043328
BLOCKS = 4


def solution(mesh):
    cols, flat = P(None, ("grp", "tile")), P(("grp", "tile"))
    return jax.shard_map(
        shards, mesh=mesh, in_specs=(cols, cols, cols, flat, flat),
        out_specs=(cols,) * 4, check_vma=False)
```

time: 129 us -> 100 us (0.78)
  the two profiles are of different devices: /device:TPU:31 before, /device:TPU:1 now
where the time goes in v2:
time: 100 us; the launch traced here: 99.9 us
  Pallas kernels  99.3 us (99%)
    pallas_call x1, Pallas kernels, shards(): pl.pallas_call(functools.partial(kernel, NG, OBS, NPTS), name='cg', out_s...  97.7 us

profile of v2, /device:TPU:1, one launch (start us, length us, event | category | flops | bytes accessed | tf_op | source)
XLA Modules:
  0.0 99.9 jit_solution(15544355416393145259)
XLA Ops:
  0.6 97.7 %cg.1 = (f32[3,4096]{1,0:T(4,128)}, f32[9,384]{1,0:T(8,128)}, f32[3,4096]{1,0:T(4,128)}, f32[9,384]{1,0:T(8,128)}) custom-call(f32[6,4096]{1,0:T(8,128)} %jp_in.1, f32[18,4096]{1,0:T(8,128)} %jc_in.1, f32[2,4096]{1,0:T(2,128)} %res_in.1, s32[1,4096]{1,0:T(1,128)} %bitcast.2, s32[1,4096]{1,0:T(1,128)} %bitcast.3), custom_call_target="tpu_custom_call" | custom-call | tf_op jit(solution)/shard_map/cg/pallas_call | solution.py:745
  98.3 1.6 %store.1 = (f32[3,4096]{1,0:T(4,128)}, f32[9,384]{1,0:T(8,128)}, f32[3,4096]{1,0:T(4,128)}, f32[9,384]{1,0:T(8,128)}) custom-call(f32[3,4096]{1,0:T(4,128)} %get-tuple-element.8.refs_0_, f32[9,384]{1,0:T(8,128)} %get-tuple-element.9.refs_1_, f32[3,4096]{1,0:T(4,128)} %get-tuple-element.10.refs_2_, f32[9,384]{1,0:T(8,128)} %get-tuple-element.11.refs_3_), custom_call_target="tpu_custom_call" | custom-call | tf_op jit(solution)/shard_map/store/pallas_call | solution.py:755

commit v3 on v2

--- a/solution.py
+++ b/solution.py
@@ -38,7 +38,7 @@
     xp_out, xc_out, rp_out, rc_out,
     jp, jc, res, pidx, cidx, in_s,
     S, R2, OHC, OHP, OHI, LHSI, LHS, LHSP, ACC, AROW, APROW, TV, TP,
-    SB0, RB0, SB, RB, VB, CV, PV, PVEC,
+    LHSF, SB, RB, VB, CV, PV, PVEC,
     PTS, PTR, XS, XR, ER, EB, G, GS, GZ, GP, XE, XEG, XQ, XQG, XV, XG,
     loc, a2a_s, a2a_r, fwd_s, fwd_r, rs_s, rs_r, ag_s, ag_r,
     pt_s, pt_r, x_s, x_r, e_s, e_r, gz_s, gz_r, gp_s, gp_r, gq_s, gq_r, pe_s, pe_r, xp, xc, rp, rc, out_s,
@@ -92,6 +92,9 @@
     final = (z, 2 * mine_k + c)
     stays = jnp.logical_and(g == z, mine_k == z)
 
+    def take(ref, sem):
+        pltpu.make_async_copy(ref, ref, sem).wait()
+
     mark("signal")
     bar = pltpu.get_barrier_semaphore()
 
@@ -127,7 +130,7 @@
 
     def a2a_copy(zt, zf):
         return pltpu.make_async_remote_copy(
-            S.at[zt], R2.at[c, zf], a2a_s.at[zt], a2a_r.at[zf],
+            S.at[zt], R2.at[c, zf], a2a_s, a2a_r.at[zf],
             device_id=(g, 2 * zt + c), device_id_type=MESH)
 
     mark("a2a_start")
@@ -187,7 +190,8 @@
                 PTS[it, i * QB + b, :, 0:SLOT] = t0[:, b * SLOT:(b + 1) * SLOT]
                 PTS[it, i * QB + b, :, SLOT:2 * SLOT] = t1[:, b * SLOT:(b + 1) * SLOT]
 
-        pltpu.make_async_copy(PTS.at[it, z], PTR.at[it, z], pt_r.at[it, z]).start()
+        pltpu.make_async_copy(
+            PTS.at[it, z], PTR.at[it, z], pt_r.at[it, lax.div(z, jnp.int32(QB))]).start()
 
         @pl.loop(1, NG)
         def _(k):
@@ -195,7 +199,7 @@
 
     def pt_copy(it, zt, zf):
         return pltpu.make_async_remote_copy(
-            PTS.at[it, zt], PTR.at[it, zf], pt_s.at[it, zt], pt_r.at[it, zf],
+            PTS.at[it, zt], PTR.at[it, zf], pt_s.at[it], pt_r.at[it, lax.div(zf, jnp.int32(QB))],
             device_id=(g, 2 * zt + c), device_id_type=MESH)
 
     mark("pt_init")
@@ -240,7 +244,7 @@
         pat_row < 16, 1, jnp.where(
             pat_row < 24, 2, jnp.where(pat_row < 27, pat_row - 24, 2000)))).astype(F32)
 
-    def cam_lhs(ref, row0, col0, v8, v1, am, t0, nt_):
+    def cam_lhs(ref, row0, col0, v8, v1, am, nt_):
         h8, l8 = split(v8)
         h1, l1 = split(v1)
         h1 = jnp.broadcast_to(h1, (8, SLOT))
@@ -248,7 +252,7 @@
         hi = jnp.concatenate([h8, h8, h8, h1], axis=0)
         lo = jnp.concatenate([l8, l8, l8, l1], axis=0)
         for t in range(nt_):
-            hit = am == float(3 * (t0 + t))
+            hit = am == float(3 * t)
             ref[row0 + t * 32:row0 + t * 32 + 32, col0:col0 + SLOT] = (
                 jnp.where(hit, hi, 0.0).astype(BF16))
             ref[row0 + nt_ * 32 + t * 32:row0 + nt_ * 32 + t * 32 + 32, col0:col0 + SLOT] = (
@@ -266,7 +270,7 @@
 
     def fwd_copy(core, zs):
         return pltpu.make_async_remote_copy(
-            R2.at[core, zs], R2.at[core, zs], fwd_s.at[zs], fwd_r.at[zs],
+            R2.at[core, zs], R2.at[core, zs], fwd_s, fwd_r.at[zs],
             device_id=partner, device_id_type=MESH)
 
     mark("cam_init")
@@ -280,49 +284,47 @@
         a2a_copy(zn, zn).wait_recv()
         fwd_copy(c, zn).start()
 
+    FB = min(6, NG // 2)
+    LB = NG - FB
+
+    def indices(zs, core, col):
+        idx = R2[core, zs, 20:21, :].astype(I32)
+        q = lax.shift_right_logical(idx, 7)
+        t = lax.shift_right_logical(q * 171, 9)
+        tau = lax.shift_right_logical(t, 1)
+        a = 3 * (tau & (T - 1)) + (q - 3 * t)
+        a = jnp.where((t & 1) == c, a, -1000).astype(F32)
+        n = (lax.shift_right_logical(tau, log_t) * 128 + (idx & 127)).astype(F32)
+        AROW[:, half_block(zs, core)] = a
+        row = lax.broadcasted_iota(I32, (256, SLOT), 0).astype(F32)
+        oh = jnp.where(row == jnp.broadcast_to(n, (256, SLOT)), 1.0, 0.0).astype(BF16)
+        OHC[:, half_block(zs, core)] = oh
+        OHI[:, col:col + SLOT] = oh
+        return a
+
     arrived(1)
 
-    @pl.loop(0, NG // 2)
+    @pl.loop(0, LB // 2)
     def _(k):
-        @pl.when(2 * k + 2 < NG)
-        def _():
-            arrived(2 * k + 2)
-            arrived(2 * k + 3)
-
-        tot = None
+        arrived(2 * k + 2)
+        arrived(2 * k + 3)
         for b in range(2):
-            zs = z_at(2 * k + b)
-            fwd_copy(1 - c, zs).wait_recv()
+            fwd_copy(1 - c, z_at(2 * k + b)).wait_recv()
         for b in range(2):
             zs = z_at(2 * k + b)
             for core in range(2):
-                idx = R2[core, zs, 20:21, :].astype(I32)
-                q = lax.shift_right_logical(idx, 7)
-                t = lax.shift_right_logical(q * 171, 9)
-                tau = lax.shift_right_logical(t, 1)
-                a = 3 * (tau & (T - 1)) + (q - 3 * t)
-                a = jnp.where((t & 1) == c, a, -1000).astype(F32)
-                n = (lax.shift_right_logical(tau, log_t) * 128 + (idx & 127)).astype(F32)
-                AROW[:, half_block(zs, core)] = a
-                row = lax.broadcasted_iota(I32, (256, SLOT), 0).astype(F32)
-                oh = jnp.where(row == jnp.broadcast_to(n, (256, SLOT)), 1.0, 0.0).astype(BF16)
-                OHC[:, half_block(zs, core)] = oh
                 col = (2 * b + core) * SLOT
-                OHI[:, col:col + SLOT] = oh
-                am = jnp.broadcast_to(a, (32, SLOT)) - pat
+                am = jnp.broadcast_to(indices(zs, core, col), (32, SLOT)) - pat
                 J0, J1, j0, j1 = jac(core, zs)
                 s0, s1 = R2[core, zs, 18:19, :], R2[core, zs, 19:20, :]
-                cam_lhs(LHSI, 0, col, -(J0 * s0 + J1 * s1), -(j0 * s0 + j1 * s1), am, 0, T)
-                cam_lhs(LHSI, 2 * ROWS, col, J0 * J0 + J1 * J1, j0 * j0 + j1 * j1, am, 0, T)
-        ACC[...] += lax.dot_general(LHSI[...], OHI[...], nt, preferred_element_type=F32)
+                cam_lhs(LHSI, 0, col, -(J0 * s0 + J1 * s1), -(j0 * s0 + j1 * s1), am, T)
+                cam_lhs(LHSI, 2 * ROWS, col, J0 * J0 + J1 * J1, j0 * j0 + j1 * j1, am, T)
+        ACC[...] += lax.dot_general(
+            LHSI[...], OHI[:, 0:4 * SLOT], nt, preferred_element_type=F32)
 
     def rs_copy(it, gt, gf, k=0):
-        if it == 2:
-            src, dst = SB0.at[k], RB0.at[gf]
-        else:
-            src, dst = SB.at[it, k], RB.at[it, gf]
-        return pltpu.make_async_remote_copy(
-            src, dst, rs_s.at[it, gt], rs_r.at[it, gf],
+        return pltpu.make_async_remote_copy(
+            SB.at[it, k], RB.at[it, gf], rs_s.at[it], rs_r.at[it],
             device_id=(gt, tt), device_id_type=MESH)
 
     def rs_send(it, k):
@@ -332,31 +334,59 @@
         def _():
             rs_copy(it, gt, g, k).start()
 
-    mark("rs_init_send")
-    for half in range(2):
-        lanes = slice(half * 128, half * 128 + 128)
-        for t in range(T):
-            for part in range(2):
-                r = 2 * ROWS * part + t * 32
-                SB0[half * T + t, part] = (
-                    ACC[r:r + 27, lanes] + ACC[r + ROWS:r + ROWS + 27, lanes])
-
-    @pl.loop(1, NG)
-    def _(d):
-        rs_send(2, chunk_of(g_at(d), z))
-
+    @pl.loop(LB + 2, NG)
+    def _(k):
+        arrived(k)
+
+    @pl.loop(LB, NG)
+    def _(k):
+        fwd_copy(1 - c, z_at(k)).wait_recv()
+
+    mark("cam_last")
+    for b in range(2 * FB):
+        indices(z_at(LB + b // 2), b % 2, b * SLOT)
+
+    @pl.loop(0, 2)
+    def _(part):
+        rhs = part == 0
+        for b in range(2 * FB):
+            zs, core = z_at(LB + b // 2), b % 2
+            J0, J1, j0, j1 = jac(core, zs)
+            s0, s1 = R2[core, zs, 18:19, :], R2[core, zs, 19:20, :]
+            f0 = jnp.where(rhs, jnp.broadcast_to(-s0, (8, SLOT)), J0)
+            f1 = jnp.where(rhs, jnp.broadcast_to(-s1, (8, SLOT)), J1)
+            g0 = jnp.where(rhs, -s0, j0)
+            g1 = jnp.where(rhs, -s1, j1)
+            am = jnp.broadcast_to(AROW[:, half_block(zs, core)], (32, SLOT)) - pat
+            cam_lhs(LHSF, 0, b * SLOT, J0 * f0 + J1 * f1, j0 * g0 + j1 * g1, am, T)
+        top = pl.multiple_of(part * (2 * ROWS), 2 * ROWS)
+        both = ACC[pl.ds(top, 2 * ROWS), :] + lax.dot_general(
+            LHSF[...], OHI[:, 0:2 * FB * SLOT], nt, preferred_element_type=F32)
+        for half in range(2):
+            lanes = slice(half * 128, half * 128 + 128)
+            for t in range(T):
+                SB[2 + part, half * T + t] = (
+                    both[t * 32:t * 32 + 27, lanes]
+                    + both[ROWS + t * 32:ROWS + t * 32 + 27, lanes])
+
+        @pl.loop(1, NG)
+        def _(d):
+            rs_send(2 + part, chunk_of(g_at(d), z))
+
+    mark("rs_init_wait")
 
     def rs_sum(it, total):
+        others = pl.ds(0, NG - 1)
+        take(RB.at[it, others], rs_r.at[it])
+
         def step(d, total):
             gf = g_at(d)
-            rs_copy(it, gf, gf).wait_recv()
-            return total + (RB0[gf] if it == 2 else RB[it, gf])
+            return total + RB[it, gf]
         return lax.fori_loop(1, NG, step, total)
 
     mark("rs_init_wait")
-    both = rs_sum(2, SB0[mine_k])
-    crhs = both[0]
-    cmat = both[1] + damping
+    crhs = rs_sum(2, SB[2, mine_k])
+    cmat = rs_sum(3, SB[3, mine_k]) + damping
     cz = crhs / cmat
     CV[0] = crhs
     CV[1] = cmat
@@ -367,7 +397,7 @@
     def ag_copy(it, gt, gf):
         k = chunk_of(gf, z)
         return pltpu.make_async_remote_copy(
-            VB.at[it, k], VB.at[it, k], ag_s.at[it, gt], ag_r.at[it, gf],
+            VB.at[it, k], VB.at[it, k], ag_s.at[it], ag_r.at[it],
             device_id=(gt, tt), device_id_type=MESH)
 
     def gather_all(it, v):
@@ -377,9 +407,7 @@
         def _(d):
             ag_copy(it, g_at(d), g).start()
 
-        @pl.loop(1, NG)
-        def _(d):
-            ag_copy(it, g_at(d), g_at(d)).wait_recv()
+        take(VB.at[it, pl.ds(0, NG - 1)], ag_r.at[it])
 
         for half in range(2):
             lanes = slice(half * 128, half * 128 + 128)
@@ -393,10 +421,12 @@
 
     NC = NG // QB
 
-    def far_first(i):
+    def order(it, k):
         if NC == 1:
-            return i
-        off = jnp.where(i == 0, 2, jnp.where(i == 1, 1, jnp.where(i == 2, 3, 0)))
+            return jnp.int32(0)
+        side = jnp.where(k == 1, 1, 3)
+        ends = (2, 0) if it == 0 else (0, 2)
+        off = jnp.where(k == 0, ends[0], jnp.where(k == 3, ends[1], side))
         return lax.rem(lax.div(z, jnp.int32(QB)) + off, jnp.int32(NC))
 
     def chunk(i):
@@ -405,22 +435,19 @@
     def x_copy(it, i):
         rows = pl.ds(2 * QB * i, 2 * QB)
         return pltpu.make_async_remote_copy(
-            XS.at[it, rows], XR.at[it, rows], x_s.at[it, i], x_r.at[it, i],
+            XS.at[it, rows], XR.at[it, rows], x_s.at[it], x_r.at[it, i],
             device_id=partner, device_id_type=MESH)
 
     def e_copy(it, zt, zf):
         return pltpu.make_async_remote_copy(
-            ER.at[it, 2 * zt + c], EB.at[it, zf], e_s.at[it, zt], e_r.at[it, zf],
+            ER.at[it, 2 * zt + c], EB.at[it, zf], e_s.at[it], e_r.at[it],
             device_id=(g, 2 * zt + c), device_id_type=MESH)
 
     def cam_errors(it):
-        @pl.loop(0, NG)
-        def _(zs):
-            pltpu.make_async_copy(PTR.at[it, zs], PTR.at[it, zs], pt_r.at[it, zs]).wait()
-
         @pl.loop(0, NC)
         def _(k):
-            i = far_first(k)
+            i = order(it, k)
+            take(PTR.at[it, pl.ds(i * QB, QB)], pt_r.at[it, i])
             got = jnp.dot(TV[...], OHC[:, chunk(i)], preferred_element_type=F32)
             for b in range(2 * QB):
                 zs, core = i * QB + b // 2, b % 2
@@ -445,11 +472,8 @@
 
             @pl.when(k > 0)
             def _():
-                errors_of(it, far_first(k - 1))
-                errors_send(it, far_first(k - 1))
-
-        mark("err")
-        errors_of(it, far_first(jnp.int32(NC - 1)))
+                errors_of(it, order(it, k - 1))
+                errors_send(it, order(it, k - 1))
 
     def errors_of(it, i):
         x_copy(it, i).wait_recv()
@@ -476,49 +500,87 @@
 
             @pl.when(zs == z)
             def _():
-                pltpu.make_async_copy(ER.at[it, 2 * z + c], EB.at[it, z], e_r.at[it, z]).start()
+                pltpu.make_async_copy(ER.at[it, 2 * z + c], EB.at[it, z], e_r.at[it]).start()
 
     NP = 2 if T > 1 else 1
     TH = T // NP
     RH = TH * 32
     WS = min(2 * QW, 2 * OBS)
 
+    def gz_copy(zt, zf):
+        return pltpu.make_async_remote_copy(
+            GS, GZ.at[zf], gz_s, gz_r,
+            device_id=(g, 2 * zt + c), device_id_type=MESH)
+
+    def last_errors(it):
+        errors_of(it, order(it, jnp.int32(NC - 1)))
+        if it == 1:
+            lane = lax.broadcasted_iota(I32, (8, 128), 1)
+            row8 = lax.broadcasted_iota(I32, (8, 128), 0)
+            each = jnp.broadcast_to(jnp.sum(G[...], axis=1, keepdims=True), (8, 128))
+            GS[...] = jnp.sum(jnp.where(lane == row8, each, 0.0), axis=0, keepdims=True)
+
+            @pl.loop(1, NG)
+            def _(k):
+                gz_copy(z_at(k), z).start()
+
+        errors_send(it, order(it, jnp.int32(NC - 1)))
+
     def cam_scatter(it):
-        for part in range(NP):
-            ACC[0:2 * RH, :] = jnp.zeros((2 * RH, 256), F32)
-
-            @pl.loop(0, 2 * OBS // WS)
-            def _(i):
-                for b in range(WS // SLOT):
-                    zs, core = i * (WS // (2 * SLOT)) + b // 2, b % 2
-                    e0 = ER[it, 2 * zs + core, :, 0:SLOT]
-                    e1 = ER[it, 2 * zs + core, :, SLOT:2 * SLOT]
-                    J0, J1, j0, j1 = jac(core, zs)
-                    am = jnp.broadcast_to(AROW[:, half_block(zs, core)], (32, SLOT)) - pat
-                    cam_lhs(LHS, 0, b * SLOT, J0 * e0 + J1 * e1, j0 * e0 + j1 * e1, am,
-                            part * TH, TH)
-                cols = pl.ds(pl.multiple_of(i * WS, WS), WS)
-                ACC[0:2 * RH, :] += lax.dot_general(
-                    LHS[...], OHC[:, cols], nt, preferred_element_type=F32)
-
-            for half in range(2):
-                lanes = slice(half * 128, half * 128 + 128)
-                for t in range(TH):
-                    SB[it, half * T + part * TH + t] = (
-                        ACC[t * 32:t * 32 + 27, lanes]
-                        + ACC[RH + t * 32:RH + t * 32 + 27, lanes])
-
-            @pl.loop(0, 2 * TH)
-            def _(d):
-                n = lax.rem(g + d, jnp.int32(2 * TH))
-                rs_send(it, lax.div(n, jnp.int32(TH)) * T + part * TH + lax.rem(n, jnp.int32(TH)))
+        steps = 2 * OBS // WS
+        tail = order(it, jnp.int32(NC - 1))
+
+        @pl.loop(0, NP * steps)
+        def _(n):
+            if steps == 1:
+                part, first, last, i = n, True, True, jnp.int32(0)
+
+                @pl.when(n == 0)
+                def _():
+                    last_errors(it)
+            else:
+                part, turn = lax.div(n, jnp.int32(2)), lax.rem(n, jnp.int32(2))
+                first, last = turn == 0, turn == 1
+                i = lax.rem(lax.div(tail, jnp.int32(2)) + 1 + turn, jnp.int32(2))
+
+                @pl.when(n == 1)
+                def _():
+                    last_errors(it)
+
+            shift = pat + (3 * TH * part).astype(F32)
+            for b in range(WS // SLOT):
+                zs, core = i * (WS // (2 * SLOT)) + b // 2, b % 2
+                e0 = ER[it, 2 * zs + core, :, 0:SLOT]
+                e1 = ER[it, 2 * zs + core, :, SLOT:2 * SLOT]
+                J0, J1, j0, j1 = jac(core, zs)
+                am = jnp.broadcast_to(AROW[:, half_block(zs, core)], (32, SLOT)) - shift
+                cam_lhs(LHS, 0, b * SLOT, J0 * e0 + J1 * e1, j0 * e0 + j1 * e1, am, TH)
+            cols = pl.ds(pl.multiple_of(i * WS, WS), WS)
+            got = lax.dot_general(LHS[...], OHC[:, cols], nt, preferred_element_type=F32)
+            ACC[0:2 * RH, :] = got + jnp.where(first, 0.0, ACC[0:2 * RH, :])
+
+            @pl.when(last)
+            def _():
+                for half in range(2):
+                    lanes = slice(half * 128, half * 128 + 128)
+                    for t in range(TH):
+                        SB[it, half * T + part * TH + t] = (
+                            ACC[t * 32:t * 32 + 27, lanes]
+                            + ACC[RH + t * 32:RH + t * 32 + 27, lanes])
+
+                @pl.loop(0, 2 * TH)
+                def _(d):
+                    m = lax.rem(g + d, jnp.int32(2 * TH))
+                    rs_send(it, lax.div(m, jnp.int32(TH)) * T + part * TH
+                            + lax.rem(m, jnp.int32(TH)))
 
     def point_scatter(it):
+        take(EB.at[it], e_r.at[it])
+
         @pl.loop(0, NG)
         def _(k):
             h = z_at(k)
             cols = pl.ds(pl.multiple_of(h * SLOT, SLOT), SLOT)
-            pltpu.make_async_copy(EB.at[it, h], EB.at[it, h], e_r.at[it, h]).wait()
             e0, e1 = EB[it, h, :, 0:SLOT], EB[it, h, :, SLOT:2 * SLOT]
             hi, lo = split(jp[0:3, cols] * e0 + jp[3:6, cols] * e1)
             v = jnp.concatenate([hi, lo, jnp.zeros((2, SLOT), F32)], axis=0)
@@ -548,8 +610,6 @@
     final_start(XE, XEG, 0)
     mark("terms0")
     cam_errors(0)
-    errors_send(0, far_first(jnp.int32(NC - 1)))
-
     mark("scat0")
     cam_scatter(0)
     mark("pscat0")
@@ -578,56 +638,39 @@
     mark("terms1")
     cam_errors(1)
 
-    def gz_copy(zt, zf):
-        return pltpu.make_async_remote_copy(
-            GS, GZ.at[zf], gz_s.at[zt], gz_r.at[zf],
-            device_id=(g, 2 * zt + c), device_id_type=MESH)
-
     def gp_copy(gt, gf):
         return pltpu.make_async_remote_copy(
-            GP.at[gf], GP.at[gf], gp_s.at[gt], gp_r.at[gf],
+            GP.at[gf], GP.at[gf], gp_s, gp_r,
             device_id=(gt, tt), device_id_type=MESH)
 
-    lane = lax.broadcasted_iota(I32, (8, 128), 1)
-    row8 = lax.broadcasted_iota(I32, (8, 128), 0)
-    each = jnp.broadcast_to(jnp.sum(G[...], axis=1, keepdims=True), (8, 128))
-    mine = jnp.sum(jnp.where(lane == row8, each, 0.0), axis=0, keepdims=True)
-    GS[...] = mine
-
-    @pl.loop(1, NG)
-    def _(k):
-        gz_copy(z_at(k), z).start()
-
-    errors_send(1, far_first(jnp.int32(NC - 1)))
     mark("scat1")
     cam_scatter(1)
-    mark("pscat1")
-    PVEC[5] = point_scatter(1) + damping * PVEC[4]
-    mark("gram_z")
-
-    def gz_step(k, total):
-        zs = z_at(k)
-        gz_copy(zs, zs).wait_recv()
-        return total + GZ[zs]
-
-    gsum = lax.fori_loop(1, NG, gz_step, mine)
-    GP[g] = gsum
-
-    @pl.loop(1, NG)
-    def _(d):
-        gp_copy(g_at(d), g).start()
-
     mark("rs1_wait")
     XV[...] = rs_sum(1, SB[1, mine_k]) + damping * CV[4]
     mark("perm")
     final_start(XV, XG, 2)
+    mark("gram_z")
+
+    def gz_step(k, total):
+        return total + GZ[z_at(k)]
+
+    take(GZ.at[pl.ds(0, NG - 1)], gz_r)
+    gsum = lax.fori_loop(1, NG, gz_step, GS[...])
+    GP[g] = gsum
+
+    @pl.loop(1, NG)
+    def _(d):
+        gp_copy(g_at(d), g).start()
+
+    mark("pscat1")
+    PVEC[5] = point_scatter(1) + damping * PVEC[4]
+
     mark("gram_p")
 
     def gp_step(d, total):
-        gf = g_at(d)
-        gp_copy(gf, gf).wait_recv()
-        return total + GP[gf]
-
+        return total + GP[g_at(d)]
+
+    take(GP.at[pl.ds(0, NG - 1)], gp_r)
     GZ[z] = lax.fori_loop(1, NG, gp_step, gsum)
     last = pltpu.make_async_remote_copy(
         GZ.at[z], GP.at[NG], gq_s, gq_r, device_id=partner, device_id_type=MESH)
@@ -664,29 +707,19 @@
     base = XEG[0] - xz * XQG[...]
 
     mark("sends")
-    @pl.loop(1, NG)
-    def _(d):
-        zt = z_at(d)
-        gt = g_at(d)
-        a2a_copy(zt, zt).wait_send()
-        gz_copy(zt, zt).wait_send()
-        for it in range(2):
-            pt_copy(it, zt, zt).wait_send()
-            e_copy(it, zt, zt).wait_send()
-            ag_copy(it, gt, gt).wait_send()
-        for it in range(3):
-            rs_copy(it, gt, gt).wait_send()
-        gp_copy(gt, gt).wait_send()
-
-    @pl.loop(0, NG)
-    def _(zs):
-        fwd_copy(c, zs).wait_send()
-
-    @pl.loop(0, NG // QB)
-    def _(i):
-        for it in range(2):
-            x_copy(it, i).wait_send()
-
+    others = pl.ds(0, NG - 1)
+    take(S.at[others], a2a_s)
+    take(R2.at[c], fwd_s)
+    take(SB.at[2, others], rs_s.at[2])
+    take(SB.at[3, others], rs_s.at[3])
+    for it in range(2):
+        take(SB.at[it, others], rs_s.at[it])
+        take(VB.at[it, others], ag_s.at[it])
+        take(PTS.at[it, others], pt_s.at[it])
+        take(XS.at[it], x_s.at[it])
+        take(ER.at[it, others], e_s.at[it])
+    take(GZ.at[others], gz_s)
+    take(GP.at[others], gp_s)
     last.wait_send()
 
     @pl.when(jnp.logical_not(stays))
@@ -719,12 +752,13 @@
         vm((1, OBS), I32), vm((1, OBS), I32), dma((5,)),
         vm((NG, 21, SLOT), F32), vm((2, NG, 21, SLOT), F32),
         vm((256, 2 * OBS), BF16), vm((256, OBS), BF16),
-        vm((256, 4 * SLOT), BF16), vm((4 * ROWS, 4 * SLOT), BF16),
+        vm((256, max(4, 2 * min(6, NG // 2)) * SLOT), BF16),
+        vm((4 * ROWS, 4 * SLOT), BF16),
         vm((2 * ROWS // min(2, T), min(4 * SLOT * QB, 2 * OBS)), BF16), vm((2 * NA * 8, OBS), BF16),
         vm((4 * ROWS, 256), F32), vm((1, 2 * OBS), F32), vm((1, OBS), F32),
         vm((2 * ROWS, 256), BF16), vm((NA * 8, 256), BF16),
-        vm((NG, 2, 27, 128), F32), vm((NG, 2, 27, 128), F32),
-        vm((2, NG, 27, 128), F32), vm((2, NG, 27, 128), F32),
+        vm((2 * ROWS, 2 * min(6, NG // 2) * SLOT), BF16),
+        vm((4, NG, 27, 128), F32), vm((4, NG, 27, 128), F32),
         vm((2, NG, 27, 128), F32), vm((5, 27, 128), F32),
         vm((8, NPTS), F32), vm((6, 3, NPTS), F32),
         vm((2, NG, 1, 2 * SLOT), F32), vm((2, NG, 1, 2 * SLOT), F32),
@@ -735,11 +769,11 @@
         vm((2, 27, 128), F32), vm((2, 27, 128), F32),
         vm((27, 128), F32), vm((27, 128), F32),
         vm((27, 128), F32), vm((27, 128), F32),
-        dma, dma((NG,)), dma((NG,)), dma((NG,)), dma((NG,)),
-        dma((3, NG)), dma((3, NG)), dma((2, NG)), dma((2, NG)),
-        dma((2, NG)), dma((2, NG)), dma((2, NG // QB)), dma((2, NG // QB)),
-        dma((2, NG)), dma((2, NG)),
-        dma((NG,)), dma((NG,)), dma((NG,)), dma((NG,)), dma, dma, dma((3,)), dma((3,)),
+        dma, dma, dma((NG,)), dma, dma((NG,)),
+        dma((4,)), dma((4,)), dma((2,)), dma((2,)),
+        dma((2,)), dma((2, NG // QB)), dma((2,)), dma((2, NG // QB)),
+        dma((2,)), dma((2,)), dma, dma, dma, dma,
+        dma, dma, dma((3,)), dma((3,)),
     ]
     outs = ((3, NPTS), (9, CAM_DEV), (3, NPTS), (9, CAM_DEV))
     made = pl.pallas_call(

time: 100 us -> 96 us (0.960)
  Pallas kernels: 99.3 us -> 95.1 us
    pallas_call x1, Pallas kernels: 97.7 us -> 93.5 us  [shards(): pl.pallas_call(functools.partial(kernel, NG, OBS, NPTS), name='cg', out_s...]
where the time goes in v3:
time: 96 us; the launch traced here: 95.8 us
  Pallas kernels  95.1 us (99%)
    pallas_call x1, Pallas kernels, shards(): pl.pallas_call(functools.partial(kernel, NG, OBS, NPTS), name='cg', out_s...  93.5 us

profile of v3, /device:TPU:1, one launch (start us, length us, event | category | flops | bytes accessed | tf_op | source)
XLA Modules:
  0.0 95.8 jit_solution(3740065409532183611)
XLA Ops:
  0.6 93.5 %cg.1 = (f32[3,4096]{1,0:T(4,128)}, f32[9,384]{1,0:T(8,128)}, f32[3,4096]{1,0:T(4,128)}, f32[9,384]{1,0:T(8,128)}) custom-call(f32[6,4096]{1,0:T(8,128)} %jp_in.1, f32[18,4096]{1,0:T(8,128)} %jc_in.1, f32[2,4096]{1,0:T(2,128)} %res_in.1, s32[1,4096]{1,0:T(1,128)} %bitcast.2, s32[1,4096]{1,0:T(1,128)} %bitcast.3), custom_call_target="tpu_custom_call" | custom-call | tf_op jit(solution)/shard_map/cg/pallas_call | solution.py:779
  94.2 1.6 %store.1 = (f32[3,4096]{1,0:T(4,128)}, f32[9,384]{1,0:T(8,128)}, f32[3,4096]{1,0:T(4,128)}, f32[9,384]{1,0:T(8,128)}) custom-call(f32[3,4096]{1,0:T(4,128)} %get-tuple-element.8.refs_0_, f32[9,384]{1,0:T(8,128)} %get-tuple-element.9.refs_1_, f32[3,4096]{1,0:T(4,128)} %get-tuple-element.10.refs_2_, f32[9,384]{1,0:T(8,128)} %get-tuple-element.11.refs_3_), custom_call_target="tpu_custom_call" | custom-call | tf_op jit(solution)/shard_map/store/pallas_call | solution.py:789

commit v4 on v3

--- a/solution.py
+++ b/solution.py
@@ -41,7 +41,7 @@
     LHSF, SB, RB, VB, CV, PV, PVEC,
     PTS, PTR, XS, XR, ER, EB, G, GS, GZ, GP, XE, XEG, XQ, XQG, XV, XG,
     loc, a2a_s, a2a_r, fwd_s, fwd_r, rs_s, rs_r, ag_s, ag_r,
-    pt_s, pt_r, x_s, x_r, e_s, e_r, gz_s, gz_r, gp_s, gp_r, gq_s, gq_r, pe_s, pe_r, xp, xc, rp, rc, out_s,
+    pt_s, pt_r, x_s, x_r, e_s, e_r, gz_s, gz_r, gp_s, gp_r, pe_s, pe_r, xp, xc, rp, rc, out_s,
 ):
     mark = Marks()
     moves = [pltpu.make_async_copy(a, b, in_s.at[i]) for i, (a, b) in enumerate((
@@ -100,8 +100,13 @@
 
     @pl.loop(1, NG)
     def _(d):
-        pl.semaphore_signal(bar, inc=1, device_id=(g, 2 * z_at(d) + c), device_id_type=MESH)
+        zf = lax.rem(z + spread(ng, ng - d), ng)
+        pl.semaphore_signal(bar, inc=1, device_id=(g, 2 * zf + c), device_id_type=MESH)
+
+    @pl.loop(1, NG)
+    def _(d):
         pl.semaphore_signal(bar, inc=1, device_id=(g_at(d), tt), device_id_type=MESH)
+        pl.semaphore_signal(bar, inc=1, device_id=(g_at(d), 2 * z + 1 - c), device_id_type=MESH)
 
     pl.semaphore_signal(bar, inc=1, device_id=partner, device_id_type=MESH)
 
@@ -126,7 +131,7 @@
     G[...] = jnp.zeros_like(G)
 
     mark("barrier")
-    pl.semaphore_wait(bar, 2 * (NG - 1) + 1 + jnp.where(stays, 0, 1))
+    pl.semaphore_wait(bar, 3 * (NG - 1) + 1 + jnp.where(stays, 0, 1))
 
     def a2a_copy(zt, zf):
         return pltpu.make_async_remote_copy(
@@ -638,10 +643,12 @@
     mark("terms1")
     cam_errors(1)
 
-    def gp_copy(gt, gf):
-        return pltpu.make_async_remote_copy(
-            GP.at[gf], GP.at[gf], gp_s, gp_r,
-            device_id=(gt, tt), device_id_type=MESH)
+    slot = c * NG + g
+
+    def gp_copy(gt, ct):
+        return pltpu.make_async_remote_copy(
+            GP.at[slot], GP.at[slot], gp_s, gp_r,
+            device_id=(gt, 2 * z + ct), device_id_type=MESH)
 
     mark("scat1")
     cam_scatter(1)
@@ -651,33 +658,24 @@
     final_start(XV, XG, 2)
     mark("gram_z")
 
-    def gz_step(k, total):
-        return total + GZ[z_at(k)]
-
     take(GZ.at[pl.ds(0, NG - 1)], gz_r)
-    gsum = lax.fori_loop(1, NG, gz_step, GS[...])
-    GP[g] = gsum
+    GZ[z] = GS[...]
+    GP[slot] = jnp.sum(GZ[...], axis=0)
+    gp_copy(g, 1 - c).start()
 
     @pl.loop(1, NG)
     def _(d):
-        gp_copy(g_at(d), g).start()
+        gp_copy(g_at(d), c).start()
+        gp_copy(g_at(d), 1 - c).start()
 
     mark("pscat1")
     PVEC[5] = point_scatter(1) + damping * PVEC[4]
 
     mark("gram_p")
 
-    def gp_step(d, total):
-        return total + GP[g_at(d)]
-
-    take(GP.at[pl.ds(0, NG - 1)], gp_r)
-    GZ[z] = lax.fori_loop(1, NG, gp_step, gsum)
-    last = pltpu.make_async_remote_copy(
-        GZ.at[z], GP.at[NG], gq_s, gq_r, device_id=partner, device_id_type=MESH)
-    last.start()
-    last.wait_recv()
+    take(GP.at[pl.ds(0, 2 * NG - 1)], gp_r)
     mark("final")
-    total = GZ[z] + GP[NG]
+    total = jnp.sum(GP[...], axis=0)
     n0, zz, ee, qw, zw, ww, eu, uu = (total[:, i:i + 1] for i in range(8))
     alpha0 = n0 / (damping * zz + ee)
     n1 = alpha0 * alpha0 * qw - n0
@@ -719,8 +717,7 @@
         take(XS.at[it], x_s.at[it])
         take(ER.at[it, others], e_s.at[it])
     take(GZ.at[others], gz_s)
-    take(GP.at[others], gp_s)
-    last.wait_send()
+    take(GP.at[pl.ds(0, 2 * NG - 1)], gp_s)
 
     @pl.when(jnp.logical_not(stays))
     def _():
@@ -765,7 +762,7 @@
         vm((2, 2 * NG, 1, 2 * SLOT), F32), vm((2, 2 * NG, 1, 2 * SLOT), F32),
         vm((2, 2 * NG, 1, 2 * SLOT), F32), vm((2, NG, 1, 2 * SLOT), F32),
         vm((8, 128), F32), vm((1, 128), F32),
-        vm((NG, 1, 128), F32), vm((NG + 1, 1, 128), F32),
+        vm((NG, 1, 128), F32), vm((2 * NG, 1, 128), F32),
         vm((2, 27, 128), F32), vm((2, 27, 128), F32),
         vm((27, 128), F32), vm((27, 128), F32),
         vm((27, 128), F32), vm((27, 128), F32),
@@ -773,7 +770,7 @@
         dma((4,)), dma((4,)), dma((2,)), dma((2,)),
         dma((2,)), dma((2, NG // QB)), dma((2,)), dma((2, NG // QB)),
         dma((2,)), dma((2,)), dma, dma, dma, dma,
-        dma, dma, dma((3,)), dma((3,)),
+        dma((3,)), dma((3,)),
     ]
     outs = ((3, NPTS), (9, CAM_DEV), (3, NPTS), (9, CAM_DEV))
     made = pl.pallas_call(

time: 96 us -> 94.9 us (0.989)
  Pallas kernels: 95.1 us -> 94.1 us
    pallas_call x1, Pallas kernels: 93.5 us -> 92.5 us  [shards(): pl.pallas_call(functools.partial(kernel, NG, OBS, NPTS), name='cg', out_s...]
where the time goes in v4:
time: 94.9 us; the launch traced here: 94.8 us
  Pallas kernels  94.1 us (99%)
    pallas_call x1, Pallas kernels, shards(): pl.pallas_call(functools.partial(kernel, NG, OBS, NPTS), name='cg', out_s...  92.5 us

profile of v4, /device:TPU:1, one launch (start us, length us, event | category | flops | bytes accessed | tf_op | source)
XLA Modules:
  0.0 94.8 jit_solution(7806972860664353138)
XLA Ops:
  0.6 92.5 %cg.1 = (f32[3,4096]{1,0:T(4,128)}, f32[9,384]{1,0:T(8,128)}, f32[3,4096]{1,0:T(4,128)}, f32[9,384]{1,0:T(8,128)}) custom-call(f32[6,4096]{1,0:T(8,128)} %jp_in.1, f32[18,4096]{1,0:T(8,128)} %jc_in.1, f32[2,4096]{1,0:T(2,128)} %res_in.1, s32[1,4096]{1,0:T(1,128)} %bitcast.2, s32[1,4096]{1,0:T(1,128)} %bitcast.3), custom_call_target="tpu_custom_call" | custom-call | tf_op jit(solution)/shard_map/cg/pallas_call | solution.py:776
  93.2 1.6 %store.1 = (f32[3,4096]{1,0:T(4,128)}, f32[9,384]{1,0:T(8,128)}, f32[3,4096]{1,0:T(4,128)}, f32[9,384]{1,0:T(8,128)}) custom-call(f32[3,4096]{1,0:T(4,128)} %get-tuple-element.8.refs_0_, f32[9,384]{1,0:T(8,128)} %get-tuple-element.9.refs_1_, f32[3,4096]{1,0:T(4,128)} %get-tuple-element.10.refs_2_, f32[9,384]{1,0:T(8,128)} %get-tuple-element.11.refs_3_), custom_call_target="tpu_custom_call" | custom-call | tf_op jit(solution)/shard_map/store/pallas_call | solution.py:786
